TPU v7x, 512 devices: a whole 4x4x16 slice. The times are simulated.
512 devices in a mesh: tm: 32 (over x_hi, z), cam: 16 (over x_lo, y, core).
Axes of the slice: x: 4 (x_hi: 2, x_lo: 2; x = x_hi * 2 + x_lo), y: 4, z: 16, core: 2. Of those that a mesh axis runs over, the one named last changes fastest.
Arguments:
- features: bfloat16 [16, 32, 64, 16, 128], P('cam', None, 'tm'), may hold values from -60 to 60
- disparity_base: int32 [1], replicated, may hold values from 0 to 3
- conv_one: float32 [4, 3, 3, 3], replicated, may hold values from -1.25 to 1.25
- conv_bias: float32 [4], replicated, may hold values from -4 to 4
- conv_two: float32 [4, 3, 3, 3], replicated, may hold values from -0.625 to 0.625
Outputs:
- disparity: float32 [16, 64, 16, 128], P('cam', 'tm')
All inputs are finite; a program needn't handle non-finite values.
Results may differ from a plain program's by a relative error of at most 0.0003.
Values may be sent and summed in bfloat16 or wider, within the bound.
No kernel may reach another device: no remote copies, remote signals or barrier semaphores. Data moves between devices by JAX's collectives and lax.ppermute only.
A program may use at most 64 MiB of HBM per device.

v0:
```python
import math

import jax
import jax.numpy as jnp
from jax import lax
from jax.sharding import PartitionSpec as P

NDISP = 32
RIG_COLS = 4


group_width = 4


def passed_along(block, axis, distance):
    devices = range(lax.axis_size(axis))
    route = [((i - distance) % len(devices), i) for i in devices]
    return lax.ppermute(block, axis, route)


def with_halo(block, sides, width):
    for axis, dim in sides:
        count = lax.axis_size(axis)
        forward = [(i, i + 1) for i in range(count - 1)]
        backward = [(target, source) for source, target in forward]
        low = lax.ppermute(
            lax.slice_in_dim(block, block.shape[dim] - width, None, axis=dim), axis, forward
        )
        high = lax.ppermute(lax.slice_in_dim(block, 0, width, axis=dim), axis, backward)
        block = jnp.concatenate([low, block, high], axis=dim)
    return block


def correlate(own_features, partner_feat, lowest, dim, sign):
    margin = NDISP + 4
    widths = [(0, 0), (0, 0), (0, 0), (0, 0)]
    widths[dim] = (margin, margin)
    padded = jnp.pad(partner_feat, tuple(widths))
    length = own_features.shape[dim]
    factor = 1.0 / math.sqrt(own_features.shape[0])

    def single(level):
        anchor = margin + sign * (lowest + level)
        window = lax.dynamic_slice_in_dim(padded, anchor, length, dim)
        return (
            jnp.einsum("cthw,cthw->thw", own_features, window, preferred_element_type=jnp.float32)
            * factor
        )

    def groups(base):
        return jax.vmap(single)(base + jnp.arange(group_width, dtype=jnp.int32))

    group_starts = jnp.arange(0, NDISP, group_width, dtype=jnp.int32)
    summed = lax.map(groups, group_starts)
    return summed.reshape((NDISP,) + own_features.shape[1:])


def first_conv(extended, conv_one, conv_bias):
    frames = extended.shape[1] - 2
    height, width_cells = (extended.shape[2], extended.shape[3])
    padded = jnp.pad(extended, ((0, 0), (0, 0), (1, 1), (1, 1)))
    summed = jnp.zeros(
        (conv_one.shape[0], extended.shape[0], frames, height, width_cells), jnp.float32
    )
    for time_lag in range(3):
        for height_lag in range(3):
            for width_lag in range(3):
                window = padded[
                    :,
                    time_lag : time_lag + frames,
                    height_lag : height_lag + height,
                    width_lag : width_lag + width_cells,
                ]
                summed = (
                    summed
                    + conv_one[:, time_lag, height_lag, width_lag][:, None, None, None, None]
                    * window[None]
                )
    return jnp.maximum(summed + conv_bias[:, None, None, None, None], 0.0)


def second_conv(extended, conv_two):
    frames = extended.shape[2] - 2
    height, width_cells = (extended.shape[3], extended.shape[4])
    padded = jnp.pad(extended, ((0, 0), (0, 0), (0, 0), (1, 1), (1, 1)))
    summed = jnp.zeros((extended.shape[1], frames, height, width_cells), jnp.float32)
    for time_lag in range(3):
        for height_lag in range(3):
            for width_lag in range(3):
                window = padded[
                    :,
                    :,
                    time_lag : time_lag + frames,
                    height_lag : height_lag + height,
                    width_lag : width_lag + width_cells,
                ]
                summed = summed + jnp.sum(
                    conv_two[:, time_lag, height_lag, width_lag][:, None, None, None, None]
                    * window,
                    axis=0,
                )
    return summed


def expected_disparity(aggregated, lowest):
    largest = jnp.max(aggregated, axis=0, keepdims=True)
    weights = jnp.exp(aggregated - largest)
    levels = (lowest + jnp.arange(NDISP, dtype=jnp.int32)).astype(jnp.float32)
    return jnp.sum(weights * levels[:, None, None, None], axis=0) / jnp.sum(weights, axis=0)


def shards(features, disparity_base, conv_one, conv_bias, conv_two):
    own_features = features[0]
    lowest = disparity_base[0]
    cameras = lax.axis_size("cam")
    row_step = cameras // RIG_COLS
    right_feat = passed_along(own_features, "cam", -1)
    down_feat = passed_along(own_features, "cam", -row_step)
    right_cost = correlate(own_features, right_feat, lowest, 3, -1)
    down_cost = correlate(own_features, down_feat, lowest, 2, -1)
    left_feat = passed_along(own_features, "cam", 1)
    up_feat = passed_along(own_features, "cam", row_step)
    left_cost = correlate(own_features, left_feat, lowest, 3, 1)
    up_cost = correlate(own_features, up_feat, lowest, 2, 1)
    summed = right_cost + left_cost + down_cost + up_cost
    cost = summed / 4.0
    group_starts = jnp.arange(0, NDISP, group_width, dtype=jnp.int32)
    extended = with_halo(cost, (("tm", 1),), 1)

    def aggregate(anchor):
        block_cost = lax.dynamic_slice_in_dim(extended, anchor, group_width, 0)
        hidden = first_conv(block_cost, conv_one, conv_bias)
        widened = with_halo(hidden, (("tm", 2),), 1)
        centre = lax.dynamic_slice_in_dim(cost, anchor, group_width, 0)
        return centre + second_conv(widened, conv_two)

    aggregated = lax.map(aggregate, group_starts).reshape(cost.shape)
    return expected_disparity(aggregated, lowest)[None]


def solution(mesh):
    in_specs = (P("cam", None, "tm", None, None), P(), P(), P(), P())
    out_specs = P("cam", "tm", None, None)
    return jax.shard_map(shards, mesh=mesh, in_specs=in_specs, out_specs=out_specs, check_vma=False)
```

profile of v0, /device:TPU:30, one launch (start us, length us, event | category | flops | bytes accessed | tf_op | source)
XLA Modules:
  0.0 487.0 jit_solution(17461747696283224265)
XLA Ops:
  7.5 5.1 %collective-permute-start.5 = (bf16[32,2,16,128]{3,2,1,0:T(8,128)(2,1)}, bf16[32,2,16,128]{3,2,1,0:T(8,128)(2,1)}, u32[]{:S(2)}, u32[]{:S(2)}) collective-permute-start(bf16[32,2,16,128]{3,2,1,0:T(8,128)(2,1)} %bitcast.216), channel_id=1, source_target_pairs={{12,0},{13,1},{14,2},{15,3},{0,4},{1,5},{2,6},{3,7},{4,8},{5,9},{6... | collective-permute-start | bytes 786440 | tf_op jit(solution)/shard_map/ppermute | solution.py:18
  15.8 106.1 %while.60 = (s32[]{:T(128)}, f32[8,4,2,16,128]{4,3,2,1,0:T(8,128)S(1)}, s32[]{:T(128)}, s32[8]{0:T(128)S(1)}, bf16[32,2,16,200]{0,2,1,3:T(8,128)(2,1)}, /*index=5*/bf16[32,2,16,128]{3,2,1,0:T(8,128)(2,1)S(1)}, s32[]{:T(128)}) while((s32[]{:T(128)}, f32[8,4,2,16,128]{4,3,2,1,0:T(8,128)S(1)}, s32[]{:T(128)}, s32[8]{0:T(128)S(1)}, ...), condition=%wide.region_1.2_spmd, body=%wide.region_0.1_spmd.sunk | while | flops 1703974 | bytes 5832885 | solution.py:54
  24.1 4.7 multiply_reduce_fusion.10
  37.4 4.7 multiply_reduce_fusion.10
  50.7 4.7 multiply_reduce_fusion.10
  77.2 4.7 multiply_reduce_fusion.10
  103.7 4.7 multiply_reduce_fusion.10
  127.0 111.7 %while.61 = (s32[]{:T(128)}, f32[8,4,2,16,128]{4,3,2,1,0:T(8,128)}, s32[]{:T(128)}, s32[8]{0:T(128)S(1)}, bf16[32,2,16,200]{0,2,1,3:T(8,128)(2,1)}, /*index=5*/bf16[32,2,16,128]{3,2,1,0:T(8,128)(2,1)S(1)}, s32[]{:T(128)}) while((s32[]{:T(128)}, f32[8,4,2,16,128]{4,3,2,1,0:T(8,128)}, s32[]{:T(128)}, s32[8]{0:T(128)S(1)}, ...), condition=%wide.region_3.4_spmd, body=%wide.region_2.3_spmd.sunk | while | flops 1703970 | bytes 5833393 | solution.py:54
  135.4 4.7 multiply_reduce_fusion.11
  191.2 4.7 multiply_reduce_fusion.11
  219.2 4.7 multiply_reduce_fusion.11
  240.9 32.8 %while.62 = (s32[]{:T(128)}, f32[8,4,2,16,128]{4,3,2,1,0:T(8,128)}, s32[]{:T(128)}, s32[8]{0:T(128)S(1)}, bf16[32,2,88,128]{3,0,1,2:T(8,128)(2,1)S(1)}, /*index=5*/bf16[32,2,16,128]{3,2,1,0:T(8,128)(2,1)S(1)}, s32[]{:T(128)}) while((s32[]{:T(128)}, f32[8,4,2,16,128]{4,3,2,1,0:T(8,128)}, s32[]{:T(128)}, s32[8]{0:T(128)S(1)}, ...), condition=%wide.region_5.6_spmd, body=%wide.region_4.5_spmd.sunk | while | flops 1703974 | bytes 5702321 | solution.py:54
  276.0 33.8 %while.63 = (s32[]{:T(128)}, f32[8,4,2,16,128]{4,3,2,1,0:T(8,128)}, s32[]{:T(128)}, s32[8]{0:T(128)S(1)}, bf16[32,2,88,128]{3,0,1,2:T(8,128)(2,1)S(1)}, /*index=5*/bf16[32,2,16,128]{3,2,1,0:T(8,128)(2,1)S(1)}, s32[]{:T(128)}) while((s32[]{:T(128)}, f32[8,4,2,16,128]{4,3,2,1,0:T(8,128)}, s32[]{:T(128)}, s32[8]{0:T(128)S(1)}, ...), condition=%wide.region_7.8_spmd, body=%wide.region_6.7_spmd.sunk | while | flops 1703970 | bytes 5702321 | solution.py:54
  315.3 10.3 %collective-permute-start.7 = (f32[32,1,16,128]{3,2,1,0:T(8,128)S(1)}, f32[32,1,16,128]{3,2,1,0:T(8,128)S(1)}, u32[]{:S(2)}, u32[]{:S(2)}) collective-permute-start(f32[32,1,16,128]{3,2,1,0:T(8,128)S(1)} %get-tuple-element.663), channel_id=1, source_target_pairs={{16,0},{32,16},{48,32},{64,48},{80,64},{96,80},{112,96},{128,112},... | collective-permute-start | bytes 786440 | tf_op jit(solution)/shard_map/ppermute | solution.py:29
  330.8 155.4 %while.64 = (s32[]{:T(128)}, f32[8,4,2,16,128]{4,3,2,1,0:T(8,128)S(1)}, s32[8]{0:T(128)S(1)}, f32[32,2,16,128]{3,2,1,0:T(8,128)S(1)}, f32[4,3,3,3]{0,3,2,1:T(4,1...) while((s32[]{:T(128)}, ...), condition=%wide.region_36.37_spmd, body=%wide.region_8.36_spmd.sunk | while | flops 9520903 | bytes 17706852 | solution.py:137
  334.5 8.0 %collective-permute-start = (f32[4,4,1,16,128]{4,3,2,1,0:T(8,128)S(1)}, f32[4,4,1,16,128]{4,3,2,1,0:T(8,128)S(1)}, u32[]{:S(2)}, u32[]{:S(2)}) collective-permute-start(f32[4,4,1,16,128]{4,3,2,1,0:T(8,128)S(1)} %get-tuple-element.1025), channel_id=1, source_target_pairs={{16,0},{32,16},{48,32},{64,48},{80,64},{96,80},{112,96},{128,112},... | collective-permute-start | bytes 393224 | tf_op jit(solution)/shard_map/while/body/eval_jaxpr/ppermute | solution.py:29
  345.9 8.3 %collective-permute-done.1 = f32[4,4,1,16,128]{4,3,2,1,0:T(8,128)S(1)} collective-permute-done((f32[4,4,1,16,128]{4,3,2,1,0:T(8,128)S(1)}, f32[4,4,1,16,128]{4,3,2,1,0:T(8,128)S(1)}, u32[]{:S(2)}, u32[]{:S(2)}) %collective-permute-start.1) | collective-permute-done | bytes 131104 | tf_op jit(solution)/shard_map/while/body/eval_jaxpr/ppermute | solution.py:26
  367.6 5.5 %collective-permute-done.1 = f32[4,4,1,16,128]{4,3,2,1,0:T(8,128)S(1)} collective-permute-done((f32[4,4,1,16,128]{4,3,2,1,0:T(8,128)S(1)}, f32[4,4,1,16,128]{4,3,2,1,0:T(8,128)S(1)}, u32[]{:S(2)}, u32[]{:S(2)}) %collective-permute-start.1) | collective-permute-done | bytes 131104 | tf_op jit(solution)/shard_map/while/body/eval_jaxpr/ppermute | solution.py:26
  386.1 5.5 %collective-permute-done.1 = f32[4,4,1,16,128]{4,3,2,1,0:T(8,128)S(1)} collective-permute-done((f32[4,4,1,16,128]{4,3,2,1,0:T(8,128)S(1)}, f32[4,4,1,16,128]{4,3,2,1,0:T(8,128)S(1)}, u32[]{:S(2)}, u32[]{:S(2)}) %collective-permute-start.1) | collective-permute-done | bytes 131104 | tf_op jit(solution)/shard_map/while/body/eval_jaxpr/ppermute | solution.py:26
  404.5 5.5 %collective-permute-done.1 = f32[4,4,1,16,128]{4,3,2,1,0:T(8,128)S(1)} collective-permute-done((f32[4,4,1,16,128]{4,3,2,1,0:T(8,128)S(1)}, f32[4,4,1,16,128]{4,3,2,1,0:T(8,128)S(1)}, u32[]{:S(2)}, u32[]{:S(2)}) %collective-permute-start.1) | collective-permute-done | bytes 131104 | tf_op jit(solution)/shard_map/while/body/eval_jaxpr/ppermute | solution.py:26
  423.0 5.5 %collective-permute-done.1 = f32[4,4,1,16,128]{4,3,2,1,0:T(8,128)S(1)} collective-permute-done((f32[4,4,1,16,128]{4,3,2,1,0:T(8,128)S(1)}, f32[4,4,1,16,128]{4,3,2,1,0:T(8,128)S(1)}, u32[]{:S(2)}, u32[]{:S(2)}) %collective-permute-start.1) | collective-permute-done | bytes 131104 | tf_op jit(solution)/shard_map/while/body/eval_jaxpr/ppermute | solution.py:26
  441.4 5.5 %collective-permute-done.1 = f32[4,4,1,16,128]{4,3,2,1,0:T(8,128)S(1)} collective-permute-done((f32[4,4,1,16,128]{4,3,2,1,0:T(8,128)S(1)}, f32[4,4,1,16,128]{4,3,2,1,0:T(8,128)S(1)}, u32[]{:S(2)}, u32[]{:S(2)}) %collective-permute-start.1) | collective-permute-done | bytes 131104 | tf_op jit(solution)/shard_map/while/body/eval_jaxpr/ppermute | solution.py:26
  459.9 5.5 %collective-permute-done.1 = f32[4,4,1,16,128]{4,3,2,1,0:T(8,128)S(1)} collective-permute-done((f32[4,4,1,16,128]{4,3,2,1,0:T(8,128)S(1)}, f32[4,4,1,16,128]{4,3,2,1,0:T(8,128)S(1)}, u32[]{:S(2)}, u32[]{:S(2)}) %collective-permute-start.1) | collective-permute-done | bytes 131104 | tf_op jit(solution)/shard_map/while/body/eval_jaxpr/ppermute | solution.py:26
  478.3 5.5 %collective-permute-done.1 = f32[4,4,1,16,128]{4,3,2,1,0:T(8,128)S(1)} collective-permute-done((f32[4,4,1,16,128]{4,3,2,1,0:T(8,128)S(1)}, f32[4,4,1,16,128]{4,3,2,1,0:T(8,128)S(1)}, u32[]{:S(2)}, u32[]{:S(2)}) %collective-permute-start.1) | collective-permute-done | bytes 131104 | tf_op jit(solution)/shard_map/while/body/eval_jaxpr/ppermute | solution.py:26
  (424 shorter events, 360.0 us)
Async XLA Ops:
  0.0 12.6 %collective-permute-start.2 = (bf16[32,2,16,128]{3,2,1,0:T(8,128)(2,1)}, bf16[32,2,16,128]{3,2,1,0:T(8,128)(2,1)S(1)}, u32[]{:S(2)}, u32[]{:S(2)}) collective-permute-start(bf16[32,2,16,128]{3,2,1,0:T(8,128)(2,1)} %bitcast.213), channel_id=1, source_target_pairs={{1,0},{2,1},{3,2},{4,3},{5,4},{6,5},{7,6},{8,7},{9,8},{10,9},{11,1... | collective-permute-start | bytes 786440 | tf_op jit(solution)/shard_map/ppermute | solution.py:18
  2.1 119.8 %collective-permute-start.3 = (bf16[32,2,16,128]{3,2,1,0:T(8,128)(2,1)}, bf16[32,2,16,128]{3,2,1,0:T(8,128)(2,1)}, u32[]{:S(2)}, u32[]{:S(2)}) collective-permute-start(bf16[32,2,16,128]{3,2,1,0:T(8,128)(2,1)} %bitcast.214), channel_id=1, source_target_pairs={{15,0},{0,1},{1,2},{2,3},{3,4},{4,5},{5,6},{6,7},{7,8},{8,9},{9,10... | collective-permute-start | bytes 786440 | tf_op jit(solution)/shard_map/ppermute | solution.py:18
  4.3 234.4 %collective-permute-start.4 = (bf16[32,2,16,128]{3,2,1,0:T(8,128)(2,1)}, bf16[32,2,16,128]{3,2,1,0:T(8,128)(2,1)}, u32[]{:S(2)}, u32[]{:S(2)}) collective-permute-start(bf16[32,2,16,128]{3,2,1,0:T(8,128)(2,1)} %bitcast.215), channel_id=1, source_target_pairs={{4,0},{5,1},{6,2},{7,3},{8,4},{9,5},{10,6},{11,7},{12,8},{13,9},{1... | collective-permute-start | bytes 786440 | tf_op jit(solution)/shard_map/ppermute | solution.py:18
  7.5 266.2 %collective-permute-start.5 = (bf16[32,2,16,128]{3,2,1,0:T(8,128)(2,1)}, bf16[32,2,16,128]{3,2,1,0:T(8,128)(2,1)}, u32[]{:S(2)}, u32[]{:S(2)}) collective-permute-start(bf16[32,2,16,128]{3,2,1,0:T(8,128)(2,1)} %bitcast.216), channel_id=1, source_target_pairs={{12,0},{13,1},{14,2},{15,3},{0,4},{1,5},{2,6},{3,7},{4,8},{5,9},{6... | collective-permute-start | bytes 786440 | tf_op jit(solution)/shard_map/ppermute | solution.py:18
  309.8 16.6 %copy-start.2 = (f32[4,3,3,3]{3,0,2,1:T(4,128)S(1)}, f32[4,3,3,3]{3,0,2,1:T(4,128)}, u32[]{:S(2)}) copy-start(f32[4,3,3,3]{3,0,2,1:T(4,128)} %param.17) | copy-start | bytes 1300
  311.4 19.4 %copy-start.3 = (f32[4]{0:T(128)S(1)}, f32[4]{0:T(128)}, u32[]{:S(2)}) copy-start(f32[4]{0:T(128)} %param.18) | copy-start | bytes 52
  311.4 17.5 %collective-permute-start.6 = (f32[32,1,16,128]{3,2,1,0:T(8,128)S(1)}, f32[32,1,16,128]{3,2,1,0:T(8,128)S(1)}, u32[]{:S(2)}, u32[]{:S(2)}) collective-permute-start(f32[32,1,16,128]{3,2,1,0:T(8,128)S(1)} %get-tuple-element.662), channel_id=1, source_target_pairs={{0,16},{16,32},{32,48},{48,64},{64,80},{80,96},{96,112},{112,128},... | collective-permute-start | bytes 786440 | tf_op jit(solution)/shard_map/ppermute | solution.py:26
  315.3 15.4 %collective-permute-start.7 = (f32[32,1,16,128]{3,2,1,0:T(8,128)S(1)}, f32[32,1,16,128]{3,2,1,0:T(8,128)S(1)}, u32[]{:S(2)}, u32[]{:S(2)}) collective-permute-start(f32[32,1,16,128]{3,2,1,0:T(8,128)S(1)} %get-tuple-element.663), channel_id=1, source_target_pairs={{16,0},{32,16},{48,32},{64,48},{80,64},{96,80},{112,96},{128,112},... | collective-permute-start | bytes 786440 | tf_op jit(solution)/shard_map/ppermute | solution.py:29
  334.5 11.4 %collective-permute-start = (f32[4,4,1,16,128]{4,3,2,1,0:T(8,128)S(1)}, f32[4,4,1,16,128]{4,3,2,1,0:T(8,128)S(1)}, u32[]{:S(2)}, u32[]{:S(2)}) collective-permute-start(f32[4,4,1,16,128]{4,3,2,1,0:T(8,128)S(1)} %get-tuple-element.1025), channel_id=1, source_target_pairs={{16,0},{32,16},{48,32},{64,48},{80,64},{96,80},{112,96},{128,112},... | collective-permute-start | bytes 393224 | tf_op jit(solution)/shard_map/while/body/eval_jaxpr/ppermute | solution.py:29
  342.5 11.7 %collective-permute-start.1 = (f32[4,4,1,16,128]{4,3,2,1,0:T(8,128)S(1)}, f32[4,4,1,16,128]{4,3,2,1,0:T(8,128)S(1)}, u32[]{:S(2)}, u32[]{:S(2)}) collective-permute-start(f32[4,4,1,16,128]{4,3,2,1,0:T(8,128)S(1)} %get-tuple-element.1026), channel_id=1, source_target_pairs={{0,16},{16,32},{32,48},{48,64},{64,80},{80,96},{96,112},{112,128},... | collective-permute-start | bytes 393224 | tf_op jit(solution)/shard_map/while/body/eval_jaxpr/ppermute | solution.py:26
  360.2 7.4 %collective-permute-start = (f32[4,4,1,16,128]{4,3,2,1,0:T(8,128)S(1)}, f32[4,4,1,16,128]{4,3,2,1,0:T(8,128)S(1)}, u32[]{:S(2)}, u32[]{:S(2)}) collective-permute-start(f32[4,4,1,16,128]{4,3,2,1,0:T(8,128)S(1)} %get-tuple-element.1025), channel_id=1, source_target_pairs={{16,0},{32,16},{48,32},{64,48},{80,64},{96,80},{112,96},{128,112},... | collective-permute-start | bytes 393224 | tf_op jit(solution)/shard_map/while/body/eval_jaxpr/ppermute | solution.py:29
  362.2 11.0 %collective-permute-start.1 = (f32[4,4,1,16,128]{4,3,2,1,0:T(8,128)S(1)}, f32[4,4,1,16,128]{4,3,2,1,0:T(8,128)S(1)}, u32[]{:S(2)}, u32[]{:S(2)}) collective-permute-start(f32[4,4,1,16,128]{4,3,2,1,0:T(8,128)S(1)} %get-tuple-element.1026), channel_id=1, source_target_pairs={{0,16},{16,32},{32,48},{48,64},{64,80},{80,96},{96,112},{112,128},... | collective-permute-start | bytes 393224 | tf_op jit(solution)/shard_map/while/body/eval_jaxpr/ppermute | solution.py:26
  379.2 6.9 %collective-permute-start = (f32[4,4,1,16,128]{4,3,2,1,0:T(8,128)S(1)}, f32[4,4,1,16,128]{4,3,2,1,0:T(8,128)S(1)}, u32[]{:S(2)}, u32[]{:S(2)}) collective-permute-start(f32[4,4,1,16,128]{4,3,2,1,0:T(8,128)S(1)} %get-tuple-element.1025), channel_id=1, source_target_pairs={{16,0},{32,16},{48,32},{64,48},{80,64},{96,80},{112,96},{128,112},... | collective-permute-start | bytes 393224 | tf_op jit(solution)/shard_map/while/body/eval_jaxpr/ppermute | solution.py:29
  381.1 10.5 %collective-permute-start.1 = (f32[4,4,1,16,128]{4,3,2,1,0:T(8,128)S(1)}, f32[4,4,1,16,128]{4,3,2,1,0:T(8,128)S(1)}, u32[]{:S(2)}, u32[]{:S(2)}) collective-permute-start(f32[4,4,1,16,128]{4,3,2,1,0:T(8,128)S(1)} %get-tuple-element.1026), channel_id=1, source_target_pairs={{0,16},{16,32},{32,48},{48,64},{64,80},{80,96},{96,112},{112,128},... | collective-permute-start | bytes 393224 | tf_op jit(solution)/shard_map/while/body/eval_jaxpr/ppermute | solution.py:26
  397.7 6.9 %collective-permute-start = (f32[4,4,1,16,128]{4,3,2,1,0:T(8,128)S(1)}, f32[4,4,1,16,128]{4,3,2,1,0:T(8,128)S(1)}, u32[]{:S(2)}, u32[]{:S(2)}) collective-permute-start(f32[4,4,1,16,128]{4,3,2,1,0:T(8,128)S(1)} %get-tuple-element.1025), channel_id=1, source_target_pairs={{16,0},{32,16},{48,32},{64,48},{80,64},{96,80},{112,96},{128,112},... | collective-permute-start | bytes 393224 | tf_op jit(solution)/shard_map/while/body/eval_jaxpr/ppermute | solution.py:29
  399.6 10.5 %collective-permute-start.1 = (f32[4,4,1,16,128]{4,3,2,1,0:T(8,128)S(1)}, f32[4,4,1,16,128]{4,3,2,1,0:T(8,128)S(1)}, u32[]{:S(2)}, u32[]{:S(2)}) collective-permute-start(f32[4,4,1,16,128]{4,3,2,1,0:T(8,128)S(1)} %get-tuple-element.1026), channel_id=1, source_target_pairs={{0,16},{16,32},{32,48},{48,64},{64,80},{80,96},{96,112},{112,128},... | collective-permute-start | bytes 393224 | tf_op jit(solution)/shard_map/while/body/eval_jaxpr/ppermute | solution.py:26
  416.1 6.9 %collective-permute-start = (f32[4,4,1,16,128]{4,3,2,1,0:T(8,128)S(1)}, f32[4,4,1,16,128]{4,3,2,1,0:T(8,128)S(1)}, u32[]{:S(2)}, u32[]{:S(2)}) collective-permute-start(f32[4,4,1,16,128]{4,3,2,1,0:T(8,128)S(1)} %get-tuple-element.1025), channel_id=1, source_target_pairs={{16,0},{32,16},{48,32},{64,48},{80,64},{96,80},{112,96},{128,112},... | collective-permute-start | bytes 393224 | tf_op jit(solution)/shard_map/while/body/eval_jaxpr/ppermute | solution.py:29
  418.0 10.5 %collective-permute-start.1 = (f32[4,4,1,16,128]{4,3,2,1,0:T(8,128)S(1)}, f32[4,4,1,16,128]{4,3,2,1,0:T(8,128)S(1)}, u32[]{:S(2)}, u32[]{:S(2)}) collective-permute-start(f32[4,4,1,16,128]{4,3,2,1,0:T(8,128)S(1)} %get-tuple-element.1026), channel_id=1, source_target_pairs={{0,16},{16,32},{32,48},{48,64},{64,80},{80,96},{96,112},{112,128},... | collective-permute-start | bytes 393224 | tf_op jit(solution)/shard_map/while/body/eval_jaxpr/ppermute | solution.py:26
  434.5 6.9 %collective-permute-start = (f32[4,4,1,16,128]{4,3,2,1,0:T(8,128)S(1)}, f32[4,4,1,16,128]{4,3,2,1,0:T(8,128)S(1)}, u32[]{:S(2)}, u32[]{:S(2)}) collective-permute-start(f32[4,4,1,16,128]{4,3,2,1,0:T(8,128)S(1)} %get-tuple-element.1025), channel_id=1, source_target_pairs={{16,0},{32,16},{48,32},{64,48},{80,64},{96,80},{112,96},{128,112},... | collective-permute-start | bytes 393224 | tf_op jit(solution)/shard_map/while/body/eval_jaxpr/ppermute | solution.py:29
  436.5 10.5 %collective-permute-start.1 = (f32[4,4,1,16,128]{4,3,2,1,0:T(8,128)S(1)}, f32[4,4,1,16,128]{4,3,2,1,0:T(8,128)S(1)}, u32[]{:S(2)}, u32[]{:S(2)}) collective-permute-start(f32[4,4,1,16,128]{4,3,2,1,0:T(8,128)S(1)} %get-tuple-element.1026), channel_id=1, source_target_pairs={{0,16},{16,32},{32,48},{48,64},{64,80},{80,96},{96,112},{112,128},... | collective-permute-start | bytes 393224 | tf_op jit(solution)/shard_map/while/body/eval_jaxpr/ppermute | solution.py:26
  453.0 6.9 %collective-permute-start = (f32[4,4,1,16,128]{4,3,2,1,0:T(8,128)S(1)}, f32[4,4,1,16,128]{4,3,2,1,0:T(8,128)S(1)}, u32[]{:S(2)}, u32[]{:S(2)}) collective-permute-start(f32[4,4,1,16,128]{4,3,2,1,0:T(8,128)S(1)} %get-tuple-element.1025), channel_id=1, source_target_pairs={{16,0},{32,16},{48,32},{64,48},{80,64},{96,80},{112,96},{128,112},... | collective-permute-start | bytes 393224 | tf_op jit(solution)/shard_map/while/body/eval_jaxpr/ppermute | solution.py:29
  454.9 10.5 %collective-permute-start.1 = (f32[4,4,1,16,128]{4,3,2,1,0:T(8,128)S(1)}, f32[4,4,1,16,128]{4,3,2,1,0:T(8,128)S(1)}, u32[]{:S(2)}, u32[]{:S(2)}) collective-permute-start(f32[4,4,1,16,128]{4,3,2,1,0:T(8,128)S(1)} %get-tuple-element.1026), channel_id=1, source_target_pairs={{0,16},{16,32},{32,48},{48,64},{64,80},{80,96},{96,112},{112,128},... | collective-permute-start | bytes 393224 | tf_op jit(solution)/shard_map/while/body/eval_jaxpr/ppermute | solution.py:26
  471.4 6.9 %collective-permute-start = (f32[4,4,1,16,128]{4,3,2,1,0:T(8,128)S(1)}, f32[4,4,1,16,128]{4,3,2,1,0:T(8,128)S(1)}, u32[]{:S(2)}, u32[]{:S(2)}) collective-permute-start(f32[4,4,1,16,128]{4,3,2,1,0:T(8,128)S(1)} %get-tuple-element.1025), channel_id=1, source_target_pairs={{16,0},{32,16},{48,32},{64,48},{80,64},{96,80},{112,96},{128,112},... | collective-permute-start | bytes 393224 | tf_op jit(solution)/shard_map/while/body/eval_jaxpr/ppermute | solution.py:29
  473.4 10.5 %collective-permute-start.1 = (f32[4,4,1,16,128]{4,3,2,1,0:T(8,128)S(1)}, f32[4,4,1,16,128]{4,3,2,1,0:T(8,128)S(1)}, u32[]{:S(2)}, u32[]{:S(2)}) collective-permute-start(f32[4,4,1,16,128]{4,3,2,1,0:T(8,128)S(1)} %get-tuple-element.1026), channel_id=1, source_target_pairs={{0,16},{16,32},{32,48},{48,64},{64,80},{80,96},{96,112},{112,128},... | collective-permute-start | bytes 393224 | tf_op jit(solution)/shard_map/while/body/eval_jaxpr/ppermute | solution.py:26
  (2 other events, 18.0 us)
where the time goes:
time: 490 us; the launch traced here: 487 us
  other arithmetic  168 us (34%)
  local copies, waits for them, and re-layouts  163 us (33%)
  starting transfers between devices  77.6 us (16%)
  waiting for transfers between devices  59.9 us (12%)
  loops' own time  17.6 us (4%)
    while x64, other arithmetic  84.5 us
    gather x32, local copies, waits for them, and re-layouts, single(): window = lax.dynamic_slice_in_dim(padded, anchor, length, dim)  83.1 us
    ppermute x9, waiting for transfers between devices, with_halo(): lax.ppermute(lax.slice_in_dim(block, block.shape[dim] - width, None, axis...  49.4 us
    concatenate x32, other arithmetic, single(): window = lax.dynamic_slice_in_dim(padded, anchor, length, dim)  42.1 us
    while x32, local copies, waits for them, and re-layouts  35.3 us
    ppermute x9, starting transfers between devices, with_halo(): lax.ppermute(lax.slice_in_dim(block, block.shape[dim] - width, None, axis...  33.2 us
    ppermute x9, starting transfers between devices, with_halo(): lax.ppermute(lax.slice_in_dim(block, 0, width, axis=dim), axis, backward)  31.8 us
    dynamic_slice x40, local copies, waits for them, and re-layouts, correlate(): summed = lax.map(groups, group_starts)  25 us
  transfers between devices with their start and end apart: 22, of which 18 were waited for; matrix products, arithmetic and copies ran while one was open for 54% of the time, Pallas kernels for 0%

commit v1 on v0

v1 whole, which is shorter than its diff:
```python
import math

import jax
import jax.numpy as jnp
from jax import lax
from jax.experimental import pallas as pl
from jax.experimental.pallas import tpu as pltpu
from jax.sharding import PartitionSpec as P

NDISP = 32
HALF = NDISP // 2
RIG_COLS = 4
HID = 4
C = 32
T = 2
H = 16
W = 128
ROWS = T * H
PITCH = ROWS + 1
GROUP = 4
LEVELS = 2
FACTOR = 1.0 / math.sqrt(C) / 4.0
F32 = jnp.float32
BF16 = jnp.bfloat16
VMEM = pl.BlockSpec(memory_space=pltpu.VMEM)
SMEM = pl.BlockSpec(memory_space=pltpu.SMEM)


def passed_along(block, axis, distance):
    count = lax.axis_size(axis)
    return lax.ppermute(block, axis, [((i - distance) % count, i) for i in range(count)])


def shifted_along(block, axis, distance):
    count = lax.axis_size(axis)
    route = [(i, i + distance) for i in range(count) if 0 <= i + distance < count]
    return lax.ppermute(block, axis, route)


def two_parts(x):
    first = x.astype(BF16)
    return first, (x - first.astype(F32)).astype(BF16)


def across_kernel(base_ref, own_ref, right_ref, left_ref, high_ref, low_ref,
                  own_s, right_s, left_s, gram_0, gram_1, horiz_s):
    base = base_ref[0]
    grams = (gram_0, gram_1)

    def widen(i, carry):
        for k in range(4):
            c = i * 4 + k
            for source, target in ((own_ref, own_s), (right_ref, right_s), (left_ref, left_s)):
                target[pl.ds(c * PITCH, ROWS), :] = source[c].reshape(ROWS, W).astype(F32)
        return carry

    lax.fori_loop(0, C // 4, widen, 0)

    row = lax.broadcasted_iota(jnp.int32, (W, W), 0)
    col = lax.broadcasted_iota(jnp.int32, (W, W), 1)
    flip = (row + col == W - 1).astype(BF16)
    same = (row == col).astype(BF16)
    lane = lax.broadcasted_iota(jnp.int32, (8, W), 1)
    sub = lax.broadcasted_iota(jnp.int32, (8, W), 0)
    nt = (((1,), (1,)), ((), ()))

    def products(g):
        def stack(source):
            return [
                source[pl.ds(g * GROUP + i, C, stride=PITCH), :].astype(BF16) for i in range(GROUP)
            ]

        rights = lax.dot_general(flip, jnp.concatenate(stack(right_s), axis=0), nt,
                                 preferred_element_type=F32).astype(BF16)
        lefts = lax.dot_general(same, jnp.concatenate(stack(left_s), axis=0), nt,
                                preferred_element_type=F32).astype(BF16)
        mine = stack(own_s)
        blank = jnp.zeros((C, W), BF16)
        blocks = jnp.concatenate(
            [
                jnp.concatenate([mine[i] if i == k else blank for k in range(GROUP)], axis=1)
                for i in range(GROUP)
            ],
            axis=0,
        )
        gram = grams[g % 2]
        gram[0:W, :] = jnp.dot(rights, blocks, preferred_element_type=F32)
        gram[W : 2 * W, :] = jnp.dot(lefts, blocks, preferred_element_type=F32)

    def diagonals(offset, read):
        low = offset & 7
        index = (sub + low) & 7
        stay = sub + low < 8
        tiles = [read(i) for i in range(W // 8)] + [jnp.zeros((8, W), F32)] * 4
        for bit, count in ((6, 12), (5, 8), (4, 6), (3, 5)):
            step = 1 << (bit - 3)
            take = (offset & (1 << bit)) != 0
            tiles = [jnp.where(take, tiles[i + step], tiles[i]) for i in range(count)]
        turned = [jnp.take_along_axis(tile, index, axis=0, mode="promise_in_bounds") for tile in tiles]
        inside = offset < W
        return [
            jnp.where(inside, jnp.where(stay, turned[i], turned[i + 1]), 0.0)
            for i in range(NDISP // 8)
        ]

    def shift(g):
        gram = grams[g % 2]
        for i in range(GROUP):
            from_right = diagonals(
                W - 1 - lane + base, lambda k: gram[8 * k : 8 * k + 8, i * W : (i + 1) * W])
            from_left = diagonals(
                lane + base, lambda k: gram[W + 8 * k : W + 8 * k + 8, i * W : (i + 1) * W])
            for k in range(NDISP // 8):
                horiz_s[pl.ds((g * GROUP + i) * PITCH + 8 * k, 8), :] = from_right[k] + from_left[k]

    groups = ROWS // GROUP
    products(0)
    for g in range(groups):
        if g + 1 < groups:
            products(g + 1)
        shift(g)

    for level in range(NDISP):
        summed = horiz_s[pl.ds(level, ROWS, stride=PITCH), :] * FACTOR
        if level < HALF:
            low_ref[level] = summed
        else:
            high_ref[level - HALF] = summed


def across(base, own, right, left):
    flat = pltpu.VMEM((C * PITCH, W), F32)
    gram = pltpu.VMEM((2 * W, GROUP * W), F32)
    half = jax.ShapeDtypeStruct((HALF, ROWS, W), F32)
    return pl.pallas_call(
        across_kernel,
        out_shape=(half, half),
        in_specs=[SMEM, VMEM, VMEM, VMEM],
        out_specs=(VMEM, VMEM),
        scratch_shapes=[flat, flat, flat, gram, gram, flat],
        compiler_params=pltpu.CompilerParams(vmem_limit_bytes=16 << 20),
        cost_estimate=pl.CostEstimate(flops=2 << 30, bytes_accessed=2 << 20, transcendentals=0),
        name="across",
    )(base, own, right, left)


def along_kernel(base_ref, low_ref, own_ref, down_ref, up_ref, cost_ref, down_s, up_s, vert_s):
    base = base_ref[0]
    half = H // 2
    zeros = jnp.zeros((H, W), F32)
    for target in (down_s, up_s):
        target[0:H, :] = zeros

    def widen(i, carry):
        for k in range(2):
            c = i * 2 + k
            for source, target in ((down_ref, down_s), (up_ref, up_s)):
                for t in range(T):
                    start = (c * T + t) * 2 * H + H
                    target[pl.ds(start, H), :] = source[c, t].astype(F32)
                    target[pl.ds(start + H, H), :] = zeros
        return carry

    lax.fori_loop(0, C // 2, widen, 0)

    for t in range(T):

        def channels(i, sums, t=t):
            for k in range(4):
                c = i * 4 + k
                mine = own_ref[c, t].astype(F32)
                mine_low, mine_high = mine[:half], mine[half:]
                start = (c * T + t) * 2 * H + H
                results = []
                for level in range(H):
                    low, high = sums[2 * level], sums[2 * level + 1]
                    part_low = up_s[pl.ds(start + level, half), :]
                    part_high = down_s[pl.ds(start + half - level, half), :]
                    if level < half:
                        part_low = part_low + down_s[pl.ds(start - level, half), :]
                        part_high = part_high + up_s[pl.ds(start + half + level, half), :]
                    results += [low + mine_low * part_low, high + mine_high * part_high]
                sums = tuple(results)
            return sums

        sums = lax.fori_loop(0, C // 4, channels,
                             tuple(jnp.zeros((half, W), F32) for _ in range(2 * H)))
        for level in range(H):
            vert_s[level, t * H : t * H + half, :] = sums[2 * level]
            vert_s[level, t * H + half : (t + 1) * H, :] = sums[2 * level + 1]
    for level in range(H, H + 4):
        vert_s[level] = jnp.zeros((ROWS, W), F32)
    for level in range(HALF):
        cost_ref[level] = low_ref[level] + vert_s[base + level] * FACTOR


def along(base, low, own, down, up):
    padded = pltpu.VMEM((C * T * 2 * H + H, W), F32)
    return pl.pallas_call(
        along_kernel,
        out_shape=jax.ShapeDtypeStruct((HALF, ROWS, W), F32),
        in_specs=[SMEM] + [VMEM] * 4,
        out_specs=VMEM,
        scratch_shapes=[padded, padded, pltpu.VMEM((H + 4, ROWS, W), F32)],
        compiler_params=pltpu.CompilerParams(vmem_limit_bytes=12 << 20),
        cost_estimate=pl.CostEstimate(flops=2 << 30, bytes_accessed=2 << 20, transcendentals=0),
        name="along",
    )(base, low, own, down, up)


def prepare_kernel(keep_ref, one_in, bias_in, two_in, one_ref, bias_ref, two_ref):
    sub = lax.broadcasted_iota(jnp.int32, (ROWS, W), 0)
    lane = lax.broadcasted_iota(jnp.int32, (ROWS, W), 1)
    frame, row = sub >> 4, sub & 15

    def taps(frame_in, row_in):
        a, b = frame_in - frame, row_in - row + 1
        valid = (a >= 0) & (a <= 2) & (b >= 0) & (b <= 2)
        return jnp.where(valid, 3 * a + b, -99)

    keeps = (
        jnp.where(frame == 0, keep_ref[0], 1.0),
        jnp.where(frame == 1, keep_ref[1], 1.0),
    )
    tap = taps((lane & 63) >> 4, lane & 15)
    for o in range(HID):
        rows = slice(o * ROWS, (o + 1) * ROWS)
        for e in range(3):
            value = jnp.zeros((ROWS, W), F32)
            for q in range(9):
                value = jnp.where(tap == q, one_in[o * 27 + q * 3 + e], value)
            for p in range(2):
                first, second = two_parts(value * keeps[p])
                one_ref[e, p, rows, 0:W] = first
                one_ref[e, p, rows, W : 2 * W] = second
        for p in range(2):
            bias_ref[p * W + o * ROWS : p * W + (o + 1) * ROWS, :] = bias_in[o] * keeps[p]
    for p in range(2):
        tap = taps(2 * p + ((lane >> 4) & 1), lane & 15) + 9 * (lane >> 5)
        code = jnp.where(taps(2 * p + ((lane >> 4) & 1), lane & 15) < 0, -1, tap)
        for e in range(3):
            value = jnp.zeros((ROWS, W), F32)
            for q in range(9 * HID):
                value = jnp.where(code == q, two_in[q * 3 + e], value)
            first, second = two_parts(value)
            for copy in range(2):
                cols = slice(copy * 2 * W + p * W, copy * 2 * W + (p + 1) * W)
                two_ref[e * ROWS : (e + 1) * ROWS, cols] = first
                two_ref[(3 + e) * ROWS : (4 + e) * ROWS, cols] = second


def prepare(keep, conv_one, conv_bias, conv_two):
    return pl.pallas_call(
        prepare_kernel,
        out_shape=(
            jax.ShapeDtypeStruct((3, 2, W, 2 * W), BF16),
            jax.ShapeDtypeStruct((2 * W, W), F32),
            jax.ShapeDtypeStruct((6 * ROWS, 4 * W), BF16),
        ),
        in_specs=[SMEM] * 4,
        out_specs=(VMEM,) * 3,
        compiler_params=pltpu.CompilerParams(vmem_limit_bytes=4 << 20),
        cost_estimate=pl.CostEstimate(flops=1 << 20, bytes_accessed=1 << 19, transcendentals=0),
        name="prepare",
    )(keep, conv_one.reshape(-1), conv_bias, conv_two.reshape(-1))


def from_left(x):
    lane = lax.broadcasted_iota(jnp.int32, (1, W), 1)
    return jnp.where(lane == 0, 0.0, pltpu.roll(x, 1, 1))


def from_right(x):
    lane = lax.broadcasted_iota(jnp.int32, (1, W), 1)
    return jnp.where(lane == W - 1, 0.0, pltpu.roll(x, W - 1, 1))


def convolve(before_ref, cost_ref, after_ref, one_ref, bias_ref, two_ref, spread, middle, write):
    steps = HALF // LEVELS

    def split(s):
        target = spread[s % 2]
        for k in range(LEVELS):
            j = s * LEVELS + k
            x = jnp.concatenate([before_ref[j], cost_ref[j], after_ref[j]], axis=0)
            for e, value in enumerate((from_left(x), x, from_right(x))):
                for q, part in enumerate(two_parts(value)):
                    target[e, q, :, k * W : (k + 1) * W] = part

    def first(s):
        source, target = spread[s % 2], middle[s % 2]
        for pair in range(2):
            rows = slice(32 * pair, 32 * pair + 64)
            total = None
            for e in range(3):
                parts = [source[e, q, rows, :] for q in range(2)]
                term = jnp.dot(one_ref[e, pair], jnp.concatenate(parts * 2, axis=0),
                               preferred_element_type=F32)
                total = term if total is None else total + term
            bias = bias_ref[W * pair : W * pair + W, :]
            hidden = jnp.maximum(total + jnp.concatenate([bias] * LEVELS, axis=1), 0.0)
            for q, part in enumerate(two_parts(hidden)):
                target[q * 2 * W + pair * W : q * 2 * W + (pair + 1) * W, :] = part

    def second(s):
        both = jnp.dot(two_ref[...], middle[s % 2][...], preferred_element_type=F32)
        both = both[: 3 * ROWS] + both[3 * ROWS :]
        for k in range(LEVELS):
            mine = both[:, k * W : (k + 1) * W]
            j = s * LEVELS + k
            write(j, cost_ref[j] + (
                from_left(mine[0:ROWS]) + mine[ROWS : 2 * ROWS] + from_right(mine[2 * ROWS :])))

    split(0)
    for s in range(steps + 1):
        if s + 1 < steps:
            split(s + 1)
        if s < steps:
            first(s)
        if s > 0:
            second(s - 1)


def high_kernel(before_ref, cost_ref, after_ref, one_ref, bias_ref, two_ref, agg_ref,
                spread_0, spread_1, middle_0, middle_1):
    def write(j, value):
        agg_ref[j] = value

    convolve(before_ref, cost_ref, after_ref, one_ref, bias_ref, two_ref,
             (spread_0, spread_1), (middle_0, middle_1), write)


def low_kernel(base_ref, before_ref, cost_ref, after_ref, one_ref, bias_ref, two_ref, high_ref,
               out_ref, spread_0, spread_1, middle_0, middle_1, agg_s):
    def write(j, value):
        agg_s[j] = value

    convolve(before_ref, cost_ref, after_ref, one_ref, bias_ref, two_ref,
             (spread_0, spread_1), (middle_0, middle_1), write)

    base = base_ref[0].astype(F32)

    def aggregated(j):
        return agg_s[j] if j < HALF else high_ref[j - HALF]

    largest = aggregated(0)
    for j in range(1, NDISP):
        largest = jnp.maximum(largest, aggregated(j))
    weight = jnp.zeros((ROWS, W), F32)
    moment = jnp.zeros((ROWS, W), F32)
    for j in range(NDISP):
        e = jnp.exp(aggregated(j) - largest)
        weight = weight + e
        moment = moment + e * (base + float(j))
    out_ref[...] = moment / weight


CONV_SCRATCH = [
    pltpu.VMEM((3, 2, 3 * ROWS, LEVELS * W), BF16),
    pltpu.VMEM((3, 2, 3 * ROWS, LEVELS * W), BF16),
    pltpu.VMEM((4 * W, LEVELS * W), BF16),
    pltpu.VMEM((4 * W, LEVELS * W), BF16),
]


def aggregate_high(before, cost, after, one, bias, two):
    return pl.pallas_call(
        high_kernel,
        out_shape=jax.ShapeDtypeStruct((HALF, ROWS, W), F32),
        in_specs=[VMEM] * 6,
        out_specs=VMEM,
        scratch_shapes=CONV_SCRATCH,
        compiler_params=pltpu.CompilerParams(vmem_limit_bytes=12 << 20),
        cost_estimate=pl.CostEstimate(flops=2 << 30, bytes_accessed=2 << 20, transcendentals=0),
        name="aggregate_high",
    )(before, cost, after, one, bias, two)


def aggregate_low(base, before, cost, after, one, bias, two, high):
    return pl.pallas_call(
        low_kernel,
        out_shape=jax.ShapeDtypeStruct((ROWS, W), F32),
        in_specs=[SMEM] + [VMEM] * 7,
        out_specs=VMEM,
        scratch_shapes=CONV_SCRATCH + [pltpu.VMEM((HALF, ROWS, W), F32)],
        compiler_params=pltpu.CompilerParams(vmem_limit_bytes=12 << 20),
        cost_estimate=pl.CostEstimate(flops=2 << 30, bytes_accessed=2 << 20, transcendentals=0),
        name="aggregate_low",
    )(base, before, cost, after, one, bias, two, high)


def shards(features, disparity_base, conv_one, conv_bias, conv_two):
    own = features[0]
    cameras = lax.axis_size("cam")
    row_step = cameras // RIG_COLS
    right = passed_along(own, "cam", -1)
    left = passed_along(own, "cam", 1)
    down = passed_along(own, "cam", -row_step)
    up = passed_along(own, "cam", row_step)
    cost_high, low = across(disparity_base, own, right, left)
    before_high = shifted_along(cost_high, "tm", 1)
    after_high = shifted_along(cost_high, "tm", -1)
    cost_low = along(disparity_base, low, own, down, up)
    before_low = shifted_along(cost_low, "tm", 1)
    after_low = shifted_along(cost_low, "tm", -1)
    conv_one, conv_bias, conv_two, _ = lax.optimization_barrier(
        (conv_one, conv_bias, conv_two, cost_low))
    place = lax.axis_index("tm")
    keep = jnp.stack([place > 0, place < lax.axis_size("tm") - 1]).astype(F32)
    one, bias, two = prepare(keep, conv_one, conv_bias, conv_two)
    high = aggregate_high(before_high, cost_high, after_high, one, bias, two)
    out = aggregate_low(disparity_base, before_low, cost_low, after_low, one, bias, two, high)
    return out.reshape(1, T, H, W)


def solution(mesh):
    in_specs = (P("cam", None, "tm", None, None), P(), P(), P(), P())
    out_specs = P("cam", "tm", None, None)
    return jax.shard_map(shards, mesh=mesh, in_specs=in_specs, out_specs=out_specs, check_vma=False)
```

time: 490 us -> 53 us (0.11)
  the two profiles are of different devices: /device:TPU:30 before, /device:TPU:4 now
where the time goes in v1:
time: 53 us; the launch traced here: 52.6 us
  starting transfers between devices  37.5 us (71%)
  Pallas kernels  9.19 us (17%)
  waiting for transfers between devices  2.64 us (5%)
  local copies, waits for them, and re-layouts  2.33 us (4%)
  between operations  0.83 us (2%)
    ppermute x4, starting transfers between devices, shifted_along(): return lax.ppermute(block, axis, route)  23.3 us
    ppermute x4, starting transfers between devices, passed_along(): lax.ppermute(block, axis, [((i - distance) % count, i) for i in range(cou...  14.2 us
    pallas_call x1, Pallas kernels, aggregate_low(): pl.pallas_call(low_kernel, out_shape=jax.ShapeDtypeStruct((ROWS, W), F32)...  2.75 us
    ppermute x4, waiting for transfers between devices, passed_along(): lax.ppermute(block, axis, [((i - distance) % count, i) for i in range(cou...  2.63 us
    unnamed x8, local copies, waits for them, and re-layouts  2.09 us
    pallas_call x1, Pallas kernels, across(): pl.pallas_call(across_kernel, out_shape=(half, half), in_specs=[SMEM, VME...  2.05 us
    pallas_call x1, Pallas kernels, aggregate_high(): pl.pallas_call(high_kernel, out_shape=jax.ShapeDtypeStruct((HALF, ROWS, W...  1.99 us
    pallas_call x1, Pallas kernels, along(): pl.pallas_call(along_kernel, out_shape=jax.ShapeDtypeStruct((HALF, ROWS,...  1.35 us
  transfers between devices with their start and end apart: 8, of which 1 were waited for; matrix products, arithmetic and copies ran while one was open for 1% of the time, Pallas kernels for 12%

profile of v1, /device:TPU:4, one launch (start us, length us, event | category | flops | bytes accessed | tf_op | source)
XLA Modules:
  0.0 52.6 jit_solution(8226277438542614473)
XLA Ops:
  0.0 5.0 %collective-permute-start = (bf16[32,2,16,128]{3,2,1,0:T(8,128)(2,1)}, bf16[32,2,16,128]{3,2,1,0:T(8,128)(2,1)S(1)}, u32[]{:S(2)}, u32[]{:S(2)}) collective-permute-start(bf16[32,2,16,128]{3,2,1,0:T(8,128)(2,1)} %bitcast.4), channel_id=1, source_target_pairs={{1,0},{2,1},{3,2},{4,3},{5,4},{6,5},{7,6},{8,7},{9,8},{10,9},{11,1... | collective-permute-start | bytes 786440 | tf_op jit(solution)/shard_map/ppermute | solution.py:31
  5.0 1.9 %collective-permute-start.1 = (bf16[32,2,16,128]{3,2,1,0:T(8,128)(2,1)}, bf16[32,2,16,128]{3,2,1,0:T(8,128)(2,1)S(1)}, u32[]{:S(2)}, u32[]{:S(2)}) collective-permute-start(bf16[32,2,16,128]{3,2,1,0:T(8,128)(2,1)} %bitcast.5), channel_id=1, source_target_pairs={{15,0},{0,1},{1,2},{2,3},{3,4},{4,5},{5,6},{6,7},{7,8},{8,9},{9,10... | collective-permute-start | bytes 786440 | tf_op jit(solution)/shard_map/ppermute | solution.py:31
  6.9 3.1 %collective-permute-start.2 = (bf16[32,2,16,128]{3,2,1,0:T(8,128)(2,1)}, bf16[32,2,16,128]{3,2,1,0:T(8,128)(2,1)S(1)}, u32[]{:S(2)}, u32[]{:S(2)}) collective-permute-start(bf16[32,2,16,128]{3,2,1,0:T(8,128)(2,1)} %bitcast.6), channel_id=1, source_target_pairs={{4,0},{5,1},{6,2},{7,3},{8,4},{9,5},{10,6},{11,7},{12,8},{13,9},{1... | collective-permute-start | bytes 786440 | tf_op jit(solution)/shard_map/ppermute | solution.py:31
  10.1 4.2 %collective-permute-start.3 = (bf16[32,2,16,128]{3,2,1,0:T(8,128)(2,1)}, bf16[32,2,16,128]{3,2,1,0:T(8,128)(2,1)S(1)}, u32[]{:S(2)}, u32[]{:S(2)}) collective-permute-start(bf16[32,2,16,128]{3,2,1,0:T(8,128)(2,1)} %bitcast.7), channel_id=1, source_target_pairs={{12,0},{13,1},{14,2},{15,3},{0,4},{1,5},{2,6},{3,7},{4,8},{5,9},{6... | collective-permute-start | bytes 786440 | tf_op jit(solution)/shard_map/ppermute | solution.py:31
  14.9 2.6 %collective-permute-done.1.left_ref = bf16[32,2,16,128]{3,2,1,0:T(8,128)(2,1)S(1)} collective-permute-done((bf16[32,2,16,128]{3,2,1,0:T(8,128)(2,1)}, bf16[32,2,16,128]{3,2,1,0:T(8,128)(2,1)S(1)}, u32[]{:S(2)}, u32[]{:S(2)}) %collective-permute-start.1) | collective-permute-done | bytes 262176 | tf_op jit(solution)/shard_map/ppermute | solution.py:31
  17.6 0.9 %copy-done = bf16[1,32,2,16,128]{4,3,2,1,0:T(8,128)(2,1)S(1)} copy-done((bf16[1,32,2,16,128]{4,3,2,1,0:T(8,128)(2,1)S(1)}, bf16[1,32,2,16,128]{4,3,2,1,0:T(8,128)(2,1)}, u32[]{:S(2)}) %copy-start) | copy-done | bytes 262168
  18.5 2.1 %across.1 = (f32[16,32,128]{2,1,0:T(8,128)S(1)}, f32[16,32,128]{2,1,0:T(8,128)S(1)}) custom-call(s32[1]{0:T(128)S(6)} %copy.10.base_ref, bf16[32,2,16,128]{3,2,1,0:T(8,128)(2,1)S(1)} %bitcast.8, bf16[32,2,16,128]{3,2,1,0:T(8,128)(2,1)S(1)} %collective-permute-done.right_ref, bf16[32,2,16,128]{3,2,1,0:T(8,128)(2,1)S(1)} %collective-permute-done.1.left_ref), custom_call_target="tpu_custom_call" | custom-call | flops 2147483648 | bytes 2097152 | tf_op jit(solution)/shard_map/across/pallas_call | solution.py:135
  20.6 3.8 %collective-permute-start.6 = (f32[16,32,128]{2,1,0:T(8,128)S(1)}, f32[16,32,128]{2,1,0:T(8,128)S(1)}, u32[]{:S(2)}, u32[]{:S(2)}) collective-permute-start(f32[16,32,128]{2,1,0:T(8,128)S(1)} %get-tuple-element.20.cost_ref), channel_id=1, source_target_pairs={{0,16},{16,32},{32,48},{48,64},{64,80},{80,96},{96,112},{112,128},... | collective-permute-start | bytes 786440 | tf_op jit(solution)/shard_map/ppermute | solution.py:37
  24.4 10.0 %collective-permute-start.7 = (f32[16,32,128]{2,1,0:T(8,128)S(1)}, f32[16,32,128]{2,1,0:T(8,128)S(1)}, u32[]{:S(2)}, u32[]{:S(2)}) collective-permute-start(f32[16,32,128]{2,1,0:T(8,128)S(1)} %get-tuple-element.20.cost_ref), channel_id=1, source_target_pairs={{16,0},{32,16},{48,32},{64,48},{80,64},{96,80},{112,96},{128,112},... | collective-permute-start | bytes 786440 | tf_op jit(solution)/shard_map/ppermute | solution.py:37
  34.4 0.0 collective-permute-done.2.down_ref
  34.4 0.0 copy-start.2
  34.4 1.4 %along.1.cost_ref = f32[16,32,128]{2,1,0:T(8,128)S(1)} custom-call(s32[1]{0:T(128)S(6)} %copy.10.base_ref, f32[16,32,128]{2,1,0:T(8,128)S(1)} %get-tuple-element.13.low_ref, bf16[32,2,16,128]{3,2,1,0:T(8,128)(2,1)S(1)} %bitcast.9, bf16[32,2,16,128]{3,2,1,0:T(8,128)(2,1)S(1)} %collective-permute-done.2.down_ref, ...), custom_call_target="tpu_custom_call" | custom-call | flops 2147483648 | bytes 2097152 | tf_op jit(solution)/shard_map/along/pallas_call | solution.py:199
  35.8 1.9 %collective-permute-start.4 = (f32[16,32,128]{2,1,0:T(8,128)S(1)}, f32[16,32,128]{2,1,0:T(8,128)S(1)}, u32[]{:S(2)}, u32[]{:S(2)}) collective-permute-start(f32[16,32,128]{2,1,0:T(8,128)S(1)} %along.1.cost_ref), channel_id=1, source_target_pairs={{0,16},{16,32},{32,48},{48,64},{64,80},{80,96},{96,112},{112,128},... | collective-permute-start | bytes 786440 | tf_op jit(solution)/shard_map/ppermute | solution.py:37
  37.7 7.5 %collective-permute-start.5 = (f32[16,32,128]{2,1,0:T(8,128)S(1)}, f32[16,32,128]{2,1,0:T(8,128)S(1)}, u32[]{:S(2)}, u32[]{:S(2)}) collective-permute-start(f32[16,32,128]{2,1,0:T(8,128)S(1)} %along.1.cost_ref), channel_id=1, source_target_pairs={{16,0},{32,16},{48,32},{64,48},{80,64},{96,80},{112,96},{128,112},... | collective-permute-start | bytes 786440 | tf_op jit(solution)/shard_map/ppermute | solution.py:37
  45.3 0.1 add_convert_fusion.keep_ref
  45.3 0.0 copy-start.3
  45.4 0.1 reshape.10.two_in
  45.5 0.6 %copy-done.3 = f32[4,3,3,3]{3,0,2,1:T(4,128)S(1)} copy-done((f32[4,3,3,3]{3,0,2,1:T(4,128)S(1)}, f32[4,3,3,3]{3,0,2,1:T(4,128)}, u32[]{:S(2)}) %copy-start.3) | copy-done | bytes 456
  46.1 0.1 reshape.9.one_in
  46.2 0.5 %copy-done.1 = f32[4]{0:T(128)S(1)} copy-done((f32[4]{0:T(128)S(1)}, f32[4]{0:T(128)}, u32[]{:S(2)}) %copy-start.1) | copy-done | bytes 40
  46.7 1.0 %prepare.1 = (bf16[3,2,128,256]{3,2,1,0:T(8,128)(2,1)S(1)}, f32[256,128]{1,0:T(8,128)S(1)}, bf16[192,512]{1,0:T(8,128)(2,1)S(1)}) custom-call(f32[2]{0:T(128)S(1)} %add_convert_fusion.keep_ref, f32[108]{0:T(128)S(1)} %reshape.9.one_in, f32[4]{0:T(128)S(1)} %copy-done.1, f32[108]{0:T(128)S(1)} %reshape.10.two_in), custom_call_target="tpu_custom_call" | custom-call | flops 1048576 | bytes 524288 | tf_op jit(solution)/shard_map/prepare/pallas_call | solution.py:253
  47.8 2.0 %aggregate_high.1.high_ref = f32[16,32,128]{2,1,0:T(8,128)S(1)} custom-call(f32[16,32,128]{2,1,0:T(8,128)S(1)} %collective-permute-done.6.before_ref, f32[16,32,128]{2,1,0:T(8,128)S(1)} %get-tuple-element.20.cost_ref, f32[16,32,128]{2,1,0:T(8,128)S(1)} %collective-permute-done.7.after_ref, bf16[3,2,128,256]{3,2,1,0:T(8,128)(2,1)S(1)} %get-tuple-element.17.one_ref, ...), custom_call_target="tpu_custom_call" | custom-call | flops 2147483648 | bytes 2097152 | tf_op jit(solution)/shard_map/aggregate_high/pallas_call | solution.py:367
  49.8 0.0 collective-permute-done.4.before_ref
  49.8 2.7 %aggregate_low.1 = f32[32,128]{1,0:T(8,128)} custom-call(s32[1]{0:T(128)S(6)} %copy.10.base_ref, f32[16,32,128]{2,1,0:T(8,128)S(1)} %collective-permute-done.4.before_ref, f32[16,32,128]{2,1,0:T(8,128)S(1)} %along.1.cost_ref, f32[16,32,128]{2,1,0:T(8,128)S(1)} %collective-permute-done.5.after_ref, bf16[3,2,128,256]{3,2,1,0:T(8,128)(2,1)S(1)} %get-tuple-element.17.one_ref, ...), custom_call_target="tpu_custom_call" | custom-call | flops 2147483648 | bytes 2097152 | tf_op jit(solution)/shard_map/aggregate_low/pallas_call | solution.py:380
  (10 shorter events, 0.0 us)
Async XLA Ops:
  0.0 14.9 %collective-permute-start = (bf16[32,2,16,128]{3,2,1,0:T(8,128)(2,1)}, bf16[32,2,16,128]{3,2,1,0:T(8,128)(2,1)S(1)}, u32[]{:S(2)}, u32[]{:S(2)}) collective-permute-start(bf16[32,2,16,128]{3,2,1,0:T(8,128)(2,1)} %bitcast.4), channel_id=1, source_target_pairs={{1,0},{2,1},{3,2},{4,3},{5,4},{6,5},{7,6},{8,7},{9,8},{10,9},{11,1... | collective-permute-start | bytes 786440 | tf_op jit(solution)/shard_map/ppermute | solution.py:31
  5.0 12.6 %collective-permute-start.1 = (bf16[32,2,16,128]{3,2,1,0:T(8,128)(2,1)}, bf16[32,2,16,128]{3,2,1,0:T(8,128)(2,1)S(1)}, u32[]{:S(2)}, u32[]{:S(2)}) collective-permute-start(bf16[32,2,16,128]{3,2,1,0:T(8,128)(2,1)} %bitcast.5), channel_id=1, source_target_pairs={{15,0},{0,1},{1,2},{2,3},{3,4},{4,5},{5,6},{6,7},{7,8},{8,9},{9,10... | collective-permute-start | bytes 786440 | tf_op jit(solution)/shard_map/ppermute | solution.py:31
  6.9 27.5 %collective-permute-start.2 = (bf16[32,2,16,128]{3,2,1,0:T(8,128)(2,1)}, bf16[32,2,16,128]{3,2,1,0:T(8,128)(2,1)S(1)}, u32[]{:S(2)}, u32[]{:S(2)}) collective-permute-start(bf16[32,2,16,128]{3,2,1,0:T(8,128)(2,1)} %bitcast.6), channel_id=1, source_target_pairs={{4,0},{5,1},{6,2},{7,3},{8,4},{9,5},{10,6},{11,7},{12,8},{13,9},{1... | collective-permute-start | bytes 786440 | tf_op jit(solution)/shard_map/ppermute | solution.py:31
  10.1 24.3 %collective-permute-start.3 = (bf16[32,2,16,128]{3,2,1,0:T(8,128)(2,1)}, bf16[32,2,16,128]{3,2,1,0:T(8,128)(2,1)S(1)}, u32[]{:S(2)}, u32[]{:S(2)}) collective-permute-start(bf16[32,2,16,128]{3,2,1,0:T(8,128)(2,1)} %bitcast.7), channel_id=1, source_target_pairs={{12,0},{13,1},{14,2},{15,3},{0,4},{1,5},{2,6},{3,7},{4,8},{5,9},{6... | collective-permute-start | bytes 786440 | tf_op jit(solution)/shard_map/ppermute | solution.py:31
  17.6 1.0 %copy-start = (bf16[1,32,2,16,128]{4,3,2,1,0:T(8,128)(2,1)S(1)}, bf16[1,32,2,16,128]{4,3,2,1,0:T(8,128)(2,1)}, u32[]{:S(2)}) copy-start(bf16[1,32,2,16,128]{4,3,2,1,0:T(8,128)(2,1)} %param.5) | copy-start | bytes 786436
  20.6 27.2 %collective-permute-start.6 = (f32[16,32,128]{2,1,0:T(8,128)S(1)}, f32[16,32,128]{2,1,0:T(8,128)S(1)}, u32[]{:S(2)}, u32[]{:S(2)}) collective-permute-start(f32[16,32,128]{2,1,0:T(8,128)S(1)} %get-tuple-element.20.cost_ref), channel_id=1, source_target_pairs={{0,16},{16,32},{32,48},{48,64},{64,80},{80,96},{96,112},{112,128},... | collective-permute-start | bytes 786440 | tf_op jit(solution)/shard_map/ppermute | solution.py:37
  24.4 23.4 %collective-permute-start.7 = (f32[16,32,128]{2,1,0:T(8,128)S(1)}, f32[16,32,128]{2,1,0:T(8,128)S(1)}, u32[]{:S(2)}, u32[]{:S(2)}) collective-permute-start(f32[16,32,128]{2,1,0:T(8,128)S(1)} %get-tuple-element.20.cost_ref), channel_id=1, source_target_pairs={{16,0},{32,16},{48,32},{64,48},{80,64},{96,80},{112,96},{128,112},... | collective-permute-start | bytes 786440 | tf_op jit(solution)/shard_map/ppermute | solution.py:37
  34.4 10.9 %copy-start.2 = (f32[4,3,3,3]{3,0,2,1:T(4,128)S(1)}, f32[4,3,3,3]{3,0,2,1:T(4,128)}, u32[]{:S(2)}) copy-start(f32[4,3,3,3]{3,0,2,1:T(4,128)} %param.9) | copy-start | bytes 1300
  35.8 14.0 %collective-permute-start.4 = (f32[16,32,128]{2,1,0:T(8,128)S(1)}, f32[16,32,128]{2,1,0:T(8,128)S(1)}, u32[]{:S(2)}, u32[]{:S(2)}) collective-permute-start(f32[16,32,128]{2,1,0:T(8,128)S(1)} %along.1.cost_ref), channel_id=1, source_target_pairs={{0,16},{16,32},{32,48},{48,64},{64,80},{80,96},{96,112},{112,128},... | collective-permute-start | bytes 786440 | tf_op jit(solution)/shard_map/ppermute | solution.py:37
  37.7 12.1 %collective-permute-start.5 = (f32[16,32,128]{2,1,0:T(8,128)S(1)}, f32[16,32,128]{2,1,0:T(8,128)S(1)}, u32[]{:S(2)}, u32[]{:S(2)}) collective-permute-start(f32[16,32,128]{2,1,0:T(8,128)S(1)} %along.1.cost_ref), channel_id=1, source_target_pairs={{16,0},{32,16},{48,32},{64,48},{80,64},{96,80},{112,96},{128,112},... | collective-permute-start | bytes 786440 | tf_op jit(solution)/shard_map/ppermute | solution.py:37
  45.3 0.7 %copy-start.3 = (f32[4,3,3,3]{3,0,2,1:T(4,128)S(1)}, f32[4,3,3,3]{3,0,2,1:T(4,128)}, u32[]{:S(2)}) copy-start(f32[4,3,3,3]{3,0,2,1:T(4,128)} %param.7) | copy-start | bytes 1300
  46.1 0.7 %copy-start.1 = (f32[4]{0:T(128)S(1)}, f32[4]{0:T(128)}, u32[]{:S(2)}) copy-start(f32[4]{0:T(128)} %bias_in) | copy-start | bytes 52

commit v2 on v1

v2 whole, which is shorter than its diff:
```python
import functools
import math

import jax
import jax.numpy as jnp
from jax import lax
from jax.experimental import pallas as pl
from jax.experimental.pallas import tpu as pltpu
from jax.sharding import PartitionSpec as P


NDISP = 32
HALF = NDISP // 2
RIG_COLS = 4
HID = 4
C = 32
T = 2
H = 16
W = 128
ROWS = T * H
PITCH = ROWS + 1
GROUP = 4
LEVELS = 2
FACTOR = 1.0 / math.sqrt(C) / 4.0
F32 = jnp.float32
BF16 = jnp.bfloat16
VMEM = pl.BlockSpec(memory_space=pltpu.VMEM)
SMEM = pl.BlockSpec(memory_space=pltpu.SMEM)
ANY = pl.BlockSpec(memory_space=pl.ANY)


def swapped(block, partner):
    return lax.ppermute(block, "cam", [(partner(k), k) for k in range(lax.axis_size("cam"))])


def shifted_along(block, axis, distance):
    count = lax.axis_size(axis)
    route = [(i, i + distance) for i in range(count) if 0 <= i + distance < count]
    return lax.ppermute(block, axis, route)


def two_parts(x):
    first = x.astype(BF16)
    return first, (x - first.astype(F32)).astype(BF16)


def widened(source, target):
    def step(i, carry):
        for k in range(4):
            c = i * 4 + k
            target[pl.ds(c * PITCH, ROWS), :] = source[c].reshape(ROWS, W).astype(F32)
        return carry

    lax.fori_loop(0, C // 4, step, 0)


def turned_group(source, g):
    return [
        source[pl.ds(g * GROUP + i, C, stride=PITCH), :].astype(BF16) for i in range(GROUP)
    ]


def correlate(base, mirrored, turned_ref, partner_s, grams, horiz_s):
    row = lax.broadcasted_iota(jnp.int32, (W, W), 0)
    col = lax.broadcasted_iota(jnp.int32, (W, W), 1)
    turn = (row == jnp.where(mirrored == 1, W - 1 - col, col)).astype(BF16)
    lane = lax.broadcasted_iota(jnp.int32, (8, W), 1)
    sub = lax.broadcasted_iota(jnp.int32, (8, W), 0)
    offset = jnp.where(mirrored == 1, W - 1 - lane, lane) + base
    index = (sub + offset) & 7
    stay = sub + (offset & 7) < 8
    inside = offset < W

    def products(g):
        partner = lax.dot_general(
            turn, jnp.concatenate(turned_group(partner_s, g), axis=0), (((1,), (1,)), ((), ())),
            preferred_element_type=F32).astype(BF16)
        mine = [turned_ref[g * W + i * C : g * W + (i + 1) * C, :] for i in range(GROUP)]
        blank = jnp.zeros((C, W), BF16)
        blocks = jnp.concatenate(
            [
                jnp.concatenate([mine[i] if i == k else blank for k in range(GROUP)], axis=1)
                for i in range(GROUP)
            ],
            axis=0,
        )
        grams[g % 2][...] = jnp.dot(partner, blocks, preferred_element_type=F32)

    def shift(g):
        gram = grams[g % 2]
        for i in range(GROUP):
            tiles = [gram[8 * k : 8 * k + 8, i * W : (i + 1) * W] for k in range(W // 8)]
            tiles += [jnp.zeros((8, W), F32)] * 4
            for bit, count in ((6, 12), (5, 8), (4, 6), (3, 5)):
                step = 1 << (bit - 3)
                take = (offset & (1 << bit)) != 0
                tiles = [jnp.where(take, tiles[k + step], tiles[k]) for k in range(count)]
            tiles = [
                jnp.take_along_axis(tile, index, axis=0, mode="promise_in_bounds") for tile in tiles
            ]
            for k in range(NDISP // 8):
                value = jnp.where(inside, jnp.where(stay, tiles[k], tiles[k + 1]), 0.0)
                horiz_s[pl.ds((g * GROUP + i) * PITCH + 8 * k, 8), :] = value

    groups = ROWS // GROUP
    products(0)
    for g in range(groups):
        if g + 1 < groups:
            products(g + 1)
        shift(g)


def near_kernel(base_ref, own_hbm, near_ref, turned_ref, part_ref,
                own_ref, sem, own_s, near_s, gram_0, gram_1, horiz_s):
    fetch = pltpu.make_async_copy(own_hbm, own_ref, sem)
    fetch.start()
    widened(near_ref, near_s)
    fetch.wait()
    widened(own_ref, own_s)
    for g in range(ROWS // GROUP):
        turned_ref[g * W : (g + 1) * W, :] = jnp.concatenate(turned_group(own_s, g), axis=0)
    correlate(base_ref[0], 1 - lax.axis_index("cam") % 2, turned_ref, near_s,
              (gram_0, gram_1), horiz_s)
    for level in range(NDISP):
        part_ref[level] = horiz_s[pl.ds(level, ROWS, stride=PITCH), :]


def next_kernel(base_ref, turned_ref, next_ref, part_ref, high_ref, low_ref,
                next_s, gram_0, gram_1, horiz_s):
    widened(next_ref, next_s)
    correlate(base_ref[0], lax.axis_index("cam") % 2, turned_ref, next_s,
              (gram_0, gram_1), horiz_s)
    for level in range(NDISP):
        summed = (part_ref[level] + horiz_s[pl.ds(level, ROWS, stride=PITCH), :]) * FACTOR
        if level < HALF:
            low_ref[level] = summed
        else:
            high_ref[level - HALF] = summed


FLAT = pltpu.VMEM((C * PITCH, W), F32)
GRAM = pltpu.VMEM((W, GROUP * W), F32)


def with_near(base, own, near):
    return pl.pallas_call(
        near_kernel,
        out_shape=(jax.ShapeDtypeStruct((ROWS * C, W), BF16),
                   jax.ShapeDtypeStruct((NDISP, ROWS, W), F32)),
        in_specs=[SMEM, ANY, VMEM],
        out_specs=(VMEM, VMEM),
        scratch_shapes=[pltpu.VMEM((C, T, H, W), BF16), pltpu.SemaphoreType.DMA,
                        FLAT, FLAT, GRAM, GRAM, FLAT],
        compiler_params=pltpu.CompilerParams(vmem_limit_bytes=12 << 20),
        cost_estimate=pl.CostEstimate(flops=1 << 30, bytes_accessed=2 << 20, transcendentals=0),
        name="with_near",
    )(base, own, near)


def with_next(base, turned, following, part):
    half = jax.ShapeDtypeStruct((HALF, ROWS, W), F32)
    return pl.pallas_call(
        next_kernel,
        out_shape=(half, half),
        in_specs=[SMEM, VMEM, VMEM, VMEM],
        out_specs=(VMEM, VMEM),
        scratch_shapes=[FLAT, GRAM, GRAM, FLAT],
        compiler_params=pltpu.CompilerParams(vmem_limit_bytes=12 << 20),
        cost_estimate=pl.CostEstimate(flops=1 << 30, bytes_accessed=2 << 20, transcendentals=0),
        name="with_next",
    )(base, turned, following, part)


def along_kernel(row_step, base_ref, own_ref, low_ref, same_ref, other_ref, cost_ref,
                 pair_s, vert_s):
    base = base_ref[0]
    half = H // 2
    size = C * T * 2 * H + H
    same_at = ((lax.axis_index("cam") // row_step) % 2) * size
    other_at = size - same_at
    zeros = jnp.zeros((H, W), F32)
    for start in (0, size):
        pair_s[start : start + H, :] = zeros

    def widen(i, carry):
        for k in range(2):
            c = i * 2 + k
            for source, at in ((same_ref, same_at), (other_ref, other_at)):
                for t in range(T):
                    start = pl.multiple_of(at + (c * T + t) * 2 * H + H, H)
                    pair_s[pl.ds(start, H), :] = source[c, t].astype(F32)
                    pair_s[pl.ds(start + H, H), :] = zeros
        return carry

    lax.fori_loop(0, C // 2, widen, 0)

    for t in range(T):

        def channels(i, sums, t=t):
            for k in range(4):
                c = i * 4 + k
                mine = own_ref[c, t].astype(F32)
                mine_low, mine_high = mine[:half], mine[half:]
                start = (c * T + t) * 2 * H + H
                results = []
                for level in range(H):
                    low, high = sums[2 * level], sums[2 * level + 1]
                    part_low = pair_s[pl.ds(size + start + level, half), :]
                    part_high = pair_s[pl.ds(start + half - level, half), :]
                    if level < half:
                        part_low = part_low + pair_s[pl.ds(start - level, half), :]
                        part_high = part_high + pair_s[pl.ds(size + start + half + level, half), :]
                    results += [low + mine_low * part_low, high + mine_high * part_high]
                sums = tuple(results)
            return sums

        sums = lax.fori_loop(0, C // 4, channels,
                             tuple(jnp.zeros((half, W), F32) for _ in range(2 * H)))
        for level in range(H):
            vert_s[level, t * H : t * H + half, :] = sums[2 * level]
            vert_s[level, t * H + half : (t + 1) * H, :] = sums[2 * level + 1]
    for level in range(H, H + 4):
        vert_s[level] = jnp.zeros((ROWS, W), F32)
    for level in range(HALF):
        cost_ref[level] = low_ref[level] + vert_s[base + level] * FACTOR


def along(row_step, base, own, low, same, other):
    padded = pltpu.VMEM((2 * (C * T * 2 * H + H), W), F32)
    return pl.pallas_call(
        functools.partial(along_kernel, row_step),
        out_shape=jax.ShapeDtypeStruct((HALF, ROWS, W), F32),
        in_specs=[SMEM] + [VMEM] * 4,
        out_specs=VMEM,
        scratch_shapes=[padded, pltpu.VMEM((H + 4, ROWS, W), F32)],
        compiler_params=pltpu.CompilerParams(vmem_limit_bytes=12 << 20),
        cost_estimate=pl.CostEstimate(flops=2 << 30, bytes_accessed=2 << 20, transcendentals=0),
        name="along",
    )(base, own, low, same, other)


def prepare_kernel(last, one_hbm, bias_hbm, two_hbm, one_ref, bias_ref, two_ref,
                   one_in, bias_in, two_in, sems):
    fetches = [
        pltpu.make_async_copy(source, target, sems.at[k])
        for k, (source, target) in enumerate(
            ((one_hbm, one_in), (bias_hbm, bias_in), (two_hbm, two_in)))
    ]
    for fetch in fetches:
        fetch.start()
    for fetch in fetches:
        fetch.wait()
    place = lax.axis_index("tm")
    keep_first = jnp.where(place > 0, 1.0, 0.0)
    keep_last = jnp.where(place < last, 1.0, 0.0)
    sub = lax.broadcasted_iota(jnp.int32, (ROWS, W), 0)
    lane = lax.broadcasted_iota(jnp.int32, (ROWS, W), 1)
    frame, row = sub >> 4, sub & 15

    def taps(frame_in, row_in):
        a, b = frame_in - frame, row_in - row + 1
        valid = (a >= 0) & (a <= 2) & (b >= 0) & (b <= 2)
        return jnp.where(valid, 3 * a + b, -99)

    keeps = (
        jnp.where(frame == 0, keep_first, 1.0),
        jnp.where(frame == 1, keep_last, 1.0),
    )
    tap = taps((lane & 63) >> 4, lane & 15)
    for o in range(HID):
        rows = slice(o * ROWS, (o + 1) * ROWS)
        for e in range(3):
            value = jnp.zeros((ROWS, W), F32)
            for q in range(9):
                value = jnp.where(tap == q, one_in[q // 3, q % 3, o, e], value)
            for p in range(2):
                first, second = two_parts(value * keeps[p])
                one_ref[e, p, rows, 0:W] = first
                one_ref[e, p, rows, W : 2 * W] = second
        for p in range(2):
            bias_ref[p * W + o * ROWS : p * W + (o + 1) * ROWS, :] = bias_in[o] * keeps[p]
    for p in range(2):
        tap = taps(2 * p + ((lane >> 4) & 1), lane & 15) + 9 * (lane >> 5)
        code = jnp.where(taps(2 * p + ((lane >> 4) & 1), lane & 15) < 0, -1, tap)
        for e in range(3):
            value = jnp.zeros((ROWS, W), F32)
            for q in range(9 * HID):
                value = jnp.where(code == q, two_in[(q % 9) // 3, q % 3, q // 9, e], value)
            first, second = two_parts(value)
            for copy in range(2):
                cols = slice(copy * W, (copy + 1) * W)
                two_ref[p, e * ROWS : (e + 1) * ROWS, cols] = first
                two_ref[p, (3 + e) * ROWS : (4 + e) * ROWS, cols] = second


def prepare(last, conv_one, conv_bias, conv_two):
    return pl.pallas_call(
        functools.partial(prepare_kernel, last),
        out_shape=(
            jax.ShapeDtypeStruct((3, 2, W, 2 * W), BF16),
            jax.ShapeDtypeStruct((2 * W, W), F32),
            jax.ShapeDtypeStruct((2, 6 * ROWS, 2 * W), BF16),
        ),
        in_specs=[ANY] * 3,
        out_specs=(VMEM,) * 3,
        scratch_shapes=[pltpu.SMEM((3, 3, HID, 3), F32), pltpu.SMEM((HID,), F32),
                        pltpu.SMEM((3, 3, HID, 3), F32), pltpu.SemaphoreType.DMA((3,))],
        compiler_params=pltpu.CompilerParams(vmem_limit_bytes=6 << 20),
        cost_estimate=pl.CostEstimate(flops=1 << 20, bytes_accessed=1 << 19, transcendentals=0),
        name="prepare",
    )(*(pltpu.with_memory_space_constraint(x, pltpu.HBM) for x in (
        conv_one.transpose(1, 2, 0, 3), conv_bias, conv_two.transpose(1, 2, 0, 3))))


def from_left(x):
    lane = lax.broadcasted_iota(jnp.int32, (1, W), 1)
    return jnp.where(lane == 0, 0.0, pltpu.roll(x, 1, 1))


def from_right(x):
    lane = lax.broadcasted_iota(jnp.int32, (1, W), 1)
    return jnp.where(lane == W - 1, 0.0, pltpu.roll(x, W - 1, 1))


def convolve(pairs, frames, one_ref, bias_ref, two_ref, scratch, write):
    steps = HALF // LEVELS
    spread, middle = scratch[:2], scratch[2:]

    def split(s):
        target = spread[s % 2]
        for k in range(LEVELS):
            x = jnp.concatenate([ref[s * LEVELS + k] for ref in frames], axis=0)
            for e, value in enumerate((from_left(x), x, from_right(x))):
                for q, part in enumerate(two_parts(value)):
                    target[e, q, 0 : len(frames) * ROWS, k * W : (k + 1) * W] = part

    def first(s):
        source, target = spread[s % 2], middle[s % 2]
        for place, pair in enumerate(pairs):
            rows = slice(ROWS * place, ROWS * place + 2 * ROWS)
            total = None
            for e in range(3):
                parts = [source[e, q, rows, :] for q in range(2)]
                term = jnp.dot(one_ref[e, pair], jnp.concatenate(parts * 2, axis=0),
                               preferred_element_type=F32)
                total = term if total is None else total + term
            bias = bias_ref[W * pair : W * pair + W, :]
            hidden = jnp.maximum(total + jnp.concatenate([bias] * LEVELS, axis=1), 0.0)
            for q, part in enumerate(two_parts(hidden)):
                target[place, q * W : (q + 1) * W, :] = part

    def second(s):
        total = None
        for place, pair in enumerate(pairs):
            term = jnp.dot(two_ref[pair], middle[s % 2][place], preferred_element_type=F32)
            total = term if total is None else total + term
        both = total[: 3 * ROWS] + total[3 * ROWS :]
        for k in range(LEVELS):
            mine = both[:, k * W : (k + 1) * W]
            write(s * LEVELS + k, (
                from_left(mine[0:ROWS]) + mine[ROWS : 2 * ROWS] + from_right(mine[2 * ROWS :])))

    split(0)
    for s in range(steps + 1):
        if s + 1 < steps:
            split(s + 1)
        if s < steps:
            first(s)
        if s > 0:
            second(s - 1)


def softened(agg_ref, lowest):
    largest = agg_ref[0]
    for j in range(1, HALF):
        largest = jnp.maximum(largest, agg_ref[j])
    weight = jnp.zeros((ROWS, W), F32)
    moment = jnp.zeros((ROWS, W), F32)
    for j in range(HALF):
        e = jnp.exp(agg_ref[j] - largest)
        weight = weight + e
        moment = moment + e * (lowest + float(j))
    return largest, weight, moment


def high_kernel(base_ref, before_ref, cost_ref, after_ref, one_ref, bias_ref, two_ref, out_ref,
                agg_s, *scratch):
    def write(j, value):
        agg_s[j] = cost_ref[j] + value

    convolve((0, 1), (before_ref, cost_ref, after_ref), one_ref, bias_ref, two_ref, scratch, write)
    lowest = base_ref[0].astype(F32) + float(HALF)
    for k, value in enumerate(softened(agg_s, lowest)):
        out_ref[k] = value


def early_kernel(before_ref, cost_ref, one_ref, bias_ref, two_ref, agg_ref, *scratch):
    def write(j, value):
        agg_ref[j] = cost_ref[j] + value

    convolve((0,), (before_ref, cost_ref), one_ref, bias_ref, two_ref, scratch, write)


def late_kernel(base_ref, cost_ref, after_ref, one_ref, bias_ref, two_ref, early_ref, high_ref,
                out_ref, agg_s, *scratch):
    def write(j, value):
        agg_s[j] = early_ref[j] + value

    convolve((1,), (cost_ref, after_ref), one_ref, bias_ref, two_ref, scratch, write)
    largest, weight, moment = softened(agg_s, base_ref[0].astype(F32))
    top = jnp.maximum(largest, high_ref[0])
    low_part, high_part = jnp.exp(largest - top), jnp.exp(high_ref[0] - top)
    weight = weight * low_part + high_ref[1] * high_part
    out_ref[...] = (moment * low_part + high_ref[2] * high_part) / weight


def conv_call(kernel, out_shape, in_specs, pairs, own_sums, *operands):
    spread = pltpu.VMEM((3, 2, (pairs + 1) * ROWS, LEVELS * W), BF16)
    middle = pltpu.VMEM((pairs, 2 * W, LEVELS * W), BF16)
    sums = [pltpu.VMEM((HALF, ROWS, W), F32)] if own_sums else []
    return pl.pallas_call(
        kernel,
        out_shape=jax.ShapeDtypeStruct(out_shape, F32),
        in_specs=in_specs,
        out_specs=VMEM,
        scratch_shapes=sums + [spread, spread, middle, middle],
        compiler_params=pltpu.CompilerParams(vmem_limit_bytes=12 << 20),
        cost_estimate=pl.CostEstimate(
            flops=pairs << 30, bytes_accessed=1 << 20, transcendentals=0),
    )(*operands)


def shards(features, disparity_base, conv_one, conv_bias, conv_two):
    own = features[0]
    cameras = lax.axis_size("cam")
    row_step = cameras // RIG_COLS
    same = swapped(own, lambda k: k ^ row_step)
    near = swapped(own, lambda k: k ^ 1)
    following = swapped(own, lambda k: (k - 1 + 2 * (k % 2)) % cameras)
    other = swapped(same, lambda k: k ^ (2 * row_step))
    turned, part = with_near(
        disparity_base, pltpu.with_memory_space_constraint(own, pltpu.HBM), near)
    cost_high, low = with_next(disparity_base, turned, following, part)
    before_high = shifted_along(cost_high, "tm", 1)
    after_high = shifted_along(cost_high, "tm", -1)
    cost_low = along(row_step, disparity_base, own, low, same, other)
    before_low = shifted_along(cost_low, "tm", 1)
    after_low = shifted_along(cost_low, "tm", -1)
    matrices = prepare(lax.axis_size("tm") - 1, conv_one, conv_bias, conv_two)
    high = conv_call(high_kernel, (3, ROWS, W), [SMEM] + [VMEM] * 6, 2, True,
                     disparity_base, before_high, cost_high, after_high, *matrices)
    early = conv_call(early_kernel, (HALF, ROWS, W), [VMEM] * 5, 1, False,
                      before_low, cost_low, *matrices)
    out = conv_call(late_kernel, (ROWS, W), [SMEM] + [VMEM] * 7, 1, True,
                    disparity_base, cost_low, after_low, *matrices, early, high)
    return out.reshape(1, T, H, W)


def solution(mesh):
    in_specs = (P("cam", None, "tm", None, None), P(), P(), P(), P())
    out_specs = P("cam", "tm", None, None)
    return jax.shard_map(shards, mesh=mesh, in_specs=in_specs, out_specs=out_specs, check_vma=False)
```

time: 53 us -> 52.6 us (level)
  the two profiles are of different devices: /device:TPU:4 before, /device:TPU:30 now
where the time goes in v2:
time: 52.6 us; the launch traced here: 52.2 us
  starting transfers between devices  33 us (63%)
  Pallas kernels  12.8 us (24%)
  waiting for transfers between devices  5.54 us (11%)
  between operations  0.82 us (2%)
    ppermute x4, starting transfers between devices, shifted_along(): return lax.ppermute(block, axis, route)  23.3 us
    ppermute x4, starting transfers between devices, swapped(): lax.ppermute(block, 'cam', [(partner(k), k) for k in range(lax.axis_size(...  9.7 us
    pallas_call x3, Pallas kernels, conv_call(): pl.pallas_call(kernel, out_shape=jax.ShapeDtypeStruct(out_shape, F32), in...  5.74 us
    ppermute x4, waiting for transfers between devices, swapped(): lax.ppermute(block, 'cam', [(partner(k), k) for k in range(lax.axis_size(...  4.65 us
    pallas_call x1, Pallas kernels, with_near(): pl.pallas_call(near_kernel, out_shape=(jax.ShapeDtypeStruct((ROWS * C, W)...  2.49 us
    pallas_call x1, Pallas kernels, prepare(): pl.pallas_call(functools.partial(prepare_kernel, last), out_shape=(jax.Sh...  1.78 us
    pallas_call x1, Pallas kernels, with_next(): pl.pallas_call(next_kernel, out_shape=(half, half), in_specs=[SMEM, VMEM,...  1.52 us
    pallas_call x1, Pallas kernels, along(): pl.pallas_call(functools.partial(along_kernel, row_step), out_shape=jax.S...  1.28 us
  transfers between devices with their start and end apart: 8, of which 2 were waited for; matrix products, arithmetic and copies ran while one was open for 0% of the time, Pallas kernels for 20%

profile of v2, /device:TPU:30, one launch (start us, length us, event | category | flops | bytes accessed | tf_op | source)
XLA Modules:
  0.0 52.2 jit_solution(6100650997740764266)
XLA Ops:
  0.0 3.1 %collective-permute-start.2 = (bf16[32,2,16,128]{3,2,1,0:T(8,128)(2,1)}, bf16[32,2,16,128]{3,2,1,0:T(8,128)(2,1)S(1)}, u32[]{:S(2)}, u32[]{:S(2)}) collective-permute-start(bf16[32,2,16,128]{3,2,1,0:T(8,128)(2,1)} %bitcast.4), channel_id=1, source_target_pairs={{4,0},{5,1},{6,2},{7,3},{0,4},{1,5},{2,6},{3,7},{12,8},{13,9},{14,... | collective-permute-start | bytes 786440 | tf_op jit(solution)/shard_map/ppermute | solution.py:33
  3.1 1.9 %collective-permute-start = (bf16[32,2,16,128]{3,2,1,0:T(8,128)(2,1)}, bf16[32,2,16,128]{3,2,1,0:T(8,128)(2,1)S(1)}, u32[]{:S(2)}, u32[]{:S(2)}) collective-permute-start(bf16[32,2,16,128]{3,2,1,0:T(8,128)(2,1)} %bitcast.5), channel_id=1, source_target_pairs={{1,0},{0,1},{3,2},{2,3},{5,4},{4,5},{7,6},{6,7},{9,8},{8,9},{11,10... | collective-permute-start | bytes 786440 | tf_op jit(solution)/shard_map/ppermute | solution.py:33
  5.1 1.9 %collective-permute-start.1 = (bf16[32,2,16,128]{3,2,1,0:T(8,128)(2,1)}, bf16[32,2,16,128]{3,2,1,0:T(8,128)(2,1)S(1)}, u32[]{:S(2)}, u32[]{:S(2)}) collective-permute-start(bf16[32,2,16,128]{3,2,1,0:T(8,128)(2,1)} %bitcast.6), channel_id=1, source_target_pairs={{15,0},{2,1},{1,2},{4,3},{3,4},{6,5},{5,6},{8,7},{7,8},{10,9},{9,1... | collective-permute-start | bytes 786440 | tf_op jit(solution)/shard_map/ppermute | solution.py:33
  7.0 4.6 %collective-permute-done.2.same_ref = bf16[32,2,16,128]{3,2,1,0:T(8,128)(2,1)S(1)} collective-permute-done((bf16[32,2,16,128]{3,2,1,0:T(8,128)(2,1)}, bf16[32,2,16,128]{3,2,1,0:T(8,128)(2,1)S(1)}, u32[]{:S(2)}, u32[]{:S(2)}) %collective-permute-start.2) | collective-permute-done | bytes 262176 | tf_op jit(solution)/shard_map/ppermute | solution.py:33
  11.6 2.7 %collective-permute-start.3 = (bf16[32,2,16,128]{3,2,1,0:T(8,128)(2,1)S(1)}, bf16[32,2,16,128]{3,2,1,0:T(8,128)(2,1)S(1)}, u32[]{:S(2)}, u32[]{:S(2)}) collective-permute-start(bf16[32,2,16,128]{3,2,1,0:T(8,128)(2,1)S(1)} %collective-permute-done.2.same_ref), channel_id=1, source_target_pairs={{8,0},{9,1},{10,2},{11,3},{12,4},{13,5},{14,6},{15,7},{0,8},{1,9},... | collective-permute-start | bytes 786440 | tf_op jit(solution)/shard_map/ppermute | solution.py:33
  15.0 0.0 collective-permute-done.near_ref
  15.0 2.5 %with_near.1 = (bf16[1024,128]{1,0:T(8,128)(2,1)S(1)}, f32[32,32,128]{2,1,0:T(8,128)S(1)}) custom-call(s32[1]{0:T(128)S(6)} %copy.6.base_ref, bf16[32,2,16,128]{3,2,1,0:T(8,128)(2,1)} %bitcast.7, bf16[32,2,16,128]{3,2,1,0:T(8,128)(2,1)S(1)} %collective-permute-done.near_ref), custom_call_target="tpu_custom_call" | custom-call | flops 1073741824 | bytes 2097152 | tf_op jit(solution)/shard_map/with_near/pallas_call | solution.py:146
  17.5 0.0 collective-permute-done.1.next_ref
  17.5 0.0 copy-start
  17.6 1.5 %with_next.1 = (f32[16,32,128]{2,1,0:T(8,128)S(1)}, f32[16,32,128]{2,1,0:T(8,128)S(1)}) custom-call(s32[1]{0:T(128)S(6)} %copy.6.base_ref, bf16[1024,128]{1,0:T(8,128)(2,1)S(1)} %get-tuple-element.12.turned_ref, bf16[32,2,16,128]{3,2,1,0:T(8,128)(2,1)S(1)} %collective-permute-done.1.next_ref, f32[32,32,128]{2,1,0:T(8,128)S(1)} %get-tuple-element.13.part_ref), custom_call_target="tpu_custom_call" | custom-call | flops 1073741824 | bytes 2097152 | tf_op jit(solution)/shard_map/with_next/pallas_call | solution.py:162
  19.1 3.8 %collective-permute-start.6 = (f32[16,32,128]{2,1,0:T(8,128)S(1)}, f32[16,32,128]{2,1,0:T(8,128)S(1)}, u32[]{:S(2)}, u32[]{:S(2)}) collective-permute-start(f32[16,32,128]{2,1,0:T(8,128)S(1)} %get-tuple-element.18.cost_ref), channel_id=1, source_target_pairs={{0,16},{16,32},{32,48},{48,64},{64,80},{80,96},{96,112},{112,128},... | collective-permute-start | bytes 786440 | tf_op jit(solution)/shard_map/ppermute | solution.py:39
  22.9 10.0 %collective-permute-start.7 = (f32[16,32,128]{2,1,0:T(8,128)S(1)}, f32[16,32,128]{2,1,0:T(8,128)S(1)}, u32[]{:S(2)}, u32[]{:S(2)}) collective-permute-start(f32[16,32,128]{2,1,0:T(8,128)S(1)} %get-tuple-element.18.cost_ref), channel_id=1, source_target_pairs={{16,0},{32,16},{48,32},{64,48},{80,64},{96,80},{112,96},{128,112},... | collective-permute-start | bytes 786440 | tf_op jit(solution)/shard_map/ppermute | solution.py:39
  33.0 0.0 collective-permute-done.3.other_ref
  33.0 1.3 %along.1.cost_ref = f32[16,32,128]{2,1,0:T(8,128)S(1)} custom-call(s32[1]{0:T(128)S(6)} %copy.6.base_ref, bf16[32,2,16,128]{3,2,1,0:T(8,128)(2,1)S(1)} %bitcast.8, f32[16,32,128]{2,1,0:T(8,128)S(1)} %get-tuple-element.14.low_ref, bf16[32,2,16,128]{3,2,1,0:T(8,128)(2,1)S(1)} %collective-permute-done.2.same_ref, ...), custom_call_target="tpu_custom_call" | custom-call | flops 2147483648 | bytes 2097152 | tf_op jit(solution)/shard_map/along/pallas_call | solution.py:230
  34.3 1.9 %collective-permute-start.5 = (f32[16,32,128]{2,1,0:T(8,128)S(1)}, f32[16,32,128]{2,1,0:T(8,128)S(1)}, u32[]{:S(2)}, u32[]{:S(2)}) collective-permute-start(f32[16,32,128]{2,1,0:T(8,128)S(1)} %along.1.cost_ref), channel_id=1, source_target_pairs={{0,16},{16,32},{32,48},{48,64},{64,80},{80,96},{96,112},{112,128},... | collective-permute-start | bytes 786440 | tf_op jit(solution)/shard_map/ppermute | solution.py:39
  36.2 1.8 %prepare.1 = (bf16[3,2,128,256]{3,2,1,0:T(8,128)(2,1)S(1)}, f32[256,128]{1,0:T(8,128)S(1)}, bf16[2,192,256]{2,1,0:T(8,128)(2,1)S(1)}) custom-call(f32[3,3,4,3]{3,2,1,0:T(4,128)} %bitcast.9, f32[4]{0:T(128)} %bias_hbm.1, f32[3,3,4,3]{3,2,1,0:T(4,128)} %bitcast.10), custom_call_target="tpu_custom_call" | custom-call | flops 1048576 | bytes 524288 | tf_op jit(solution)/shard_map/prepare/pallas_call | solution.py:297
  38.0 7.5 %collective-permute-start.4 = (f32[16,32,128]{2,1,0:T(8,128)S(1)}, f32[16,32,128]{2,1,0:T(8,128)S(1)}, u32[]{:S(2)}, u32[]{:S(2)}) collective-permute-start(f32[16,32,128]{2,1,0:T(8,128)S(1)} %along.1.cost_ref), channel_id=1, source_target_pairs={{16,0},{32,16},{48,32},{64,48},{80,64},{96,80},{112,96},{128,112},... | collective-permute-start | bytes 786440 | tf_op jit(solution)/shard_map/ppermute | solution.py:39
  45.5 0.0 collective-permute-done.6.before_ref
  45.5 0.0 collective-permute-done.7.after_ref
  45.6 2.0 %shard_map.56.high_ref = f32[3,32,128]{2,1,0:T(8,128)S(1)} custom-call(s32[1]{0:T(128)S(6)} %copy.6.base_ref, f32[16,32,128]{2,1,0:T(8,128)S(1)} %collective-permute-done.6.before_ref, f32[16,32,128]{2,1,0:T(8,128)S(1)} %get-tuple-element.18.cost_ref, f32[16,32,128]{2,1,0:T(8,128)S(1)} %collective-permute-done.7.after_ref, ...), custom_call_target="tpu_custom_call" | custom-call | flops 2147483648 | bytes 1048576 | tf_op jit(solution)/shard_map/pallas_call | solution.py:421
  47.6 0.0 collective-permute-done.5.before_ref
  47.6 1.5 %shard_map.55.early_ref = f32[16,32,128]{2,1,0:T(8,128)S(1)} custom-call(f32[16,32,128]{2,1,0:T(8,128)S(1)} %collective-permute-done.5.before_ref, f32[16,32,128]{2,1,0:T(8,128)S(1)} %along.1.cost_ref, bf16[3,2,128,256]{3,2,1,0:T(8,128)(2,1)S(1)} %get-tuple-element.15.one_ref, f32[256,128]{1,0:T(8,128)S(1)} %get-tuple-element.16.bias_ref, ...), custom_call_target="tpu_custom_call" | custom-call | flops 1073741824 | bytes 1048576 | tf_op jit(solution)/shard_map/pallas_call | solution.py:421
  49.1 0.9 %collective-permute-done.4.after_ref = f32[16,32,128]{2,1,0:T(8,128)S(1)} collective-permute-done((f32[16,32,128]{2,1,0:T(8,128)S(1)}, f32[16,32,128]{2,1,0:T(8,128)S(1)}, u32[]{:S(2)}, u32[]{:S(2)}) %collective-permute-start.4) | collective-permute-done | bytes 262176 | tf_op jit(solution)/shard_map/ppermute | solution.py:39
  50.0 2.2 %shard_map.57 = f32[32,128]{1,0:T(8,128)} custom-call(s32[1]{0:T(128)S(6)} %copy.6.base_ref, f32[16,32,128]{2,1,0:T(8,128)S(1)} %along.1.cost_ref, f32[16,32,128]{2,1,0:T(8,128)S(1)} %collective-permute-done.4.after_ref, bf16[3,2,128,256]{3,2,1,0:T(8,128)(2,1)S(1)} %get-tuple-element.15.one_ref, f32[256,128]{1,0:T(8,128)S(1)} %get-tuple-element.16.bias_ref, ...), custom_call_target="tpu_custom_call" | custom-call | flops 1073741824 | bytes 1048576 | tf_op jit(solution)/shard_map/pallas_call | solution.py:421
  (1 shorter events, 0.0 us)
Async XLA Ops:
  0.0 11.6 %collective-permute-start.2 = (bf16[32,2,16,128]{3,2,1,0:T(8,128)(2,1)}, bf16[32,2,16,128]{3,2,1,0:T(8,128)(2,1)S(1)}, u32[]{:S(2)}, u32[]{:S(2)}) collective-permute-start(bf16[32,2,16,128]{3,2,1,0:T(8,128)(2,1)} %bitcast.4), channel_id=1, source_target_pairs={{4,0},{5,1},{6,2},{7,3},{0,4},{1,5},{2,6},{3,7},{12,8},{13,9},{14,... | collective-permute-start | bytes 786440 | tf_op jit(solution)/shard_map/ppermute | solution.py:33
  3.1 11.9 %collective-permute-start = (bf16[32,2,16,128]{3,2,1,0:T(8,128)(2,1)}, bf16[32,2,16,128]{3,2,1,0:T(8,128)(2,1)S(1)}, u32[]{:S(2)}, u32[]{:S(2)}) collective-permute-start(bf16[32,2,16,128]{3,2,1,0:T(8,128)(2,1)} %bitcast.5), channel_id=1, source_target_pairs={{1,0},{0,1},{3,2},{2,3},{5,4},{4,5},{7,6},{6,7},{9,8},{8,9},{11,10... | collective-permute-start | bytes 786440 | tf_op jit(solution)/shard_map/ppermute | solution.py:33
  5.1 12.5 %collective-permute-start.1 = (bf16[32,2,16,128]{3,2,1,0:T(8,128)(2,1)}, bf16[32,2,16,128]{3,2,1,0:T(8,128)(2,1)S(1)}, u32[]{:S(2)}, u32[]{:S(2)}) collective-permute-start(bf16[32,2,16,128]{3,2,1,0:T(8,128)(2,1)} %bitcast.6), channel_id=1, source_target_pairs={{15,0},{2,1},{1,2},{4,3},{3,4},{6,5},{5,6},{8,7},{7,8},{10,9},{9,1... | collective-permute-start | bytes 786440 | tf_op jit(solution)/shard_map/ppermute | solution.py:33
  11.6 21.3 %collective-permute-start.3 = (bf16[32,2,16,128]{3,2,1,0:T(8,128)(2,1)S(1)}, bf16[32,2,16,128]{3,2,1,0:T(8,128)(2,1)S(1)}, u32[]{:S(2)}, u32[]{:S(2)}) collective-permute-start(bf16[32,2,16,128]{3,2,1,0:T(8,128)(2,1)S(1)} %collective-permute-done.2.same_ref), channel_id=1, source_target_pairs={{8,0},{9,1},{10,2},{11,3},{12,4},{13,5},{14,6},{15,7},{0,8},{1,9},... | collective-permute-start | bytes 786440 | tf_op jit(solution)/shard_map/ppermute | solution.py:33
  17.5 15.4 %copy-start = (bf16[1,32,2,16,128]{4,3,2,1,0:T(8,128)(2,1)S(1)}, bf16[1,32,2,16,128]{4,3,2,1,0:T(8,128)(2,1)}, u32[]{:S(2)}) copy-start(bf16[1,32,2,16,128]{4,3,2,1,0:T(8,128)(2,1)} %param.5) | copy-start | bytes 786436
  19.1 26.5 %collective-permute-start.6 = (f32[16,32,128]{2,1,0:T(8,128)S(1)}, f32[16,32,128]{2,1,0:T(8,128)S(1)}, u32[]{:S(2)}, u32[]{:S(2)}) collective-permute-start(f32[16,32,128]{2,1,0:T(8,128)S(1)} %get-tuple-element.18.cost_ref), channel_id=1, source_target_pairs={{0,16},{16,32},{32,48},{48,64},{64,80},{80,96},{96,112},{112,128},... | collective-permute-start | bytes 786440 | tf_op jit(solution)/shard_map/ppermute | solution.py:39
  22.9 22.6 %collective-permute-start.7 = (f32[16,32,128]{2,1,0:T(8,128)S(1)}, f32[16,32,128]{2,1,0:T(8,128)S(1)}, u32[]{:S(2)}, u32[]{:S(2)}) collective-permute-start(f32[16,32,128]{2,1,0:T(8,128)S(1)} %get-tuple-element.18.cost_ref), channel_id=1, source_target_pairs={{16,0},{32,16},{48,32},{64,48},{80,64},{96,80},{112,96},{128,112},... | collective-permute-start | bytes 786440 | tf_op jit(solution)/shard_map/ppermute | solution.py:39
  34.3 13.3 %collective-permute-start.5 = (f32[16,32,128]{2,1,0:T(8,128)S(1)}, f32[16,32,128]{2,1,0:T(8,128)S(1)}, u32[]{:S(2)}, u32[]{:S(2)}) collective-permute-start(f32[16,32,128]{2,1,0:T(8,128)S(1)} %along.1.cost_ref), channel_id=1, source_target_pairs={{0,16},{16,32},{32,48},{48,64},{64,80},{80,96},{96,112},{112,128},... | collective-permute-start | bytes 786440 | tf_op jit(solution)/shard_map/ppermute | solution.py:39
  38.0 12.0 %collective-permute-start.4 = (f32[16,32,128]{2,1,0:T(8,128)S(1)}, f32[16,32,128]{2,1,0:T(8,128)S(1)}, u32[]{:S(2)}, u32[]{:S(2)}) collective-permute-start(f32[16,32,128]{2,1,0:T(8,128)S(1)} %along.1.cost_ref), channel_id=1, source_target_pairs={{16,0},{32,16},{48,32},{64,48},{80,64},{96,80},{112,96},{128,112},... | collective-permute-start | bytes 786440 | tf_op jit(solution)/shard_map/ppermute | solution.py:39

commit v3 on v2

--- a/solution.py
+++ b/solution.py
@@ -18,9 +18,10 @@
 H = 16
 W = 128
 ROWS = T * H
+HALF_WORDS = HALF // 4 * 3 * ROWS
 PITCH = ROWS + 1
 GROUP = 4
-LEVELS = 2
+LEVELS = 8
 FACTOR = 1.0 / math.sqrt(C) / 4.0
 F32 = jnp.float32
 BF16 = jnp.bfloat16
@@ -42,6 +43,62 @@
 def two_parts(x):
     first = x.astype(BF16)
     return first, (x - first.astype(F32)).astype(BF16)
+
+
+LOWEST_POWER, HIGHEST_POWER = -24, 15
+
+
+def largest_of(planes):
+    top = jnp.abs(planes[0])
+    for plane in planes[1:]:
+        top = jnp.maximum(top, jnp.abs(plane))
+    return jnp.broadcast_to(jnp.max(top, axis=(0, 1), keepdims=True), (8, W))
+
+
+def power_of(top):
+    power = jnp.full((8, W), LOWEST_POWER - 1, jnp.int32)
+    for k in range(LOWEST_POWER, HIGHEST_POWER + 1):
+        power = jnp.where(top >= 2.0**k, k, power)
+    return power
+
+
+def by_power(power, sign, bits):
+    factor = jnp.full((8, W), 2.0 ** (sign * (bits - LOWEST_POWER + 1)), F32)
+    for k in range(LOWEST_POWER, HIGHEST_POWER + 1):
+        factor = jnp.where(power >= k, 2.0 ** (sign * (bits - k)), factor)
+    return jnp.concatenate([factor] * (ROWS // 8), axis=0)
+
+
+def packed(planes, power):
+    factor = by_power(power, 1, 22)
+    words = []
+    for i in range(0, len(planes), 4):
+        q = [
+            jnp.minimum(jnp.floor(plane * factor + 0.5), 2.0**23 - 1).astype(jnp.int32)
+            for plane in planes[i : i + 4]
+        ]
+        last = (q[3] & 255, (q[3] >> 8) & 255, (q[3] >> 16) & 255)
+        words += [(q[k] << 8) | last[k] for k in range(3)]
+    return words
+
+
+def unpack(source, start, power_at, target, place, levels):
+    factor = by_power(source[power_at : power_at + 8, :], -1, 22)
+    for i in range(0, levels, 4):
+        at = start + i // 4 * 3 * ROWS
+        words = [source[at + k * ROWS : at + (k + 1) * ROWS, :] for k in range(3)]
+        last = ((words[2] & 255) << 24) | ((words[1] & 255) << 16) | ((words[0] & 255) << 8)
+        for k, q in enumerate([word >> 8 for word in words] + [last >> 8]):
+            target[place + i + k] = q.astype(F32) * factor
+
+
+def put(target, start, words):
+    for k, word in enumerate(words):
+        target[start + k * ROWS : start + (k + 1) * ROWS, :] = word
+
+
+def coded(levels, powers=1):
+    return jax.ShapeDtypeStruct((levels // 4 * 3 * ROWS + 8 * powers, W), jnp.int32)
 
 
 def widened(source, target):
@@ -125,7 +182,7 @@
         part_ref[level] = horiz_s[pl.ds(level, ROWS, stride=PITCH), :]
 
 
-def next_kernel(base_ref, turned_ref, next_ref, part_ref, high_ref, low_ref,
+def next_kernel(base_ref, turned_ref, next_ref, part_ref, high_ref, low_ref, code_ref,
                 next_s, gram_0, gram_1, horiz_s):
     widened(next_ref, next_s)
     correlate(base_ref[0], lax.axis_index("cam") % 2, turned_ref, next_s,
@@ -136,6 +193,10 @@
             low_ref[level] = summed
         else:
             high_ref[level - HALF] = summed
+    planes = [high_ref[k] for k in range(HALF)]
+    power = power_of(largest_of(planes))
+    put(code_ref, 0, packed(planes, power))
+    code_ref[HALF_WORDS : HALF_WORDS + 8, :] = power
 
 
 FLAT = pltpu.VMEM((C * PITCH, W), F32)
@@ -161,9 +222,9 @@
     half = jax.ShapeDtypeStruct((HALF, ROWS, W), F32)
     return pl.pallas_call(
         next_kernel,
-        out_shape=(half, half),
+        out_shape=(half, half, coded(HALF)),
         in_specs=[SMEM, VMEM, VMEM, VMEM],
-        out_specs=(VMEM, VMEM),
+        out_specs=(VMEM, VMEM, VMEM),
         scratch_shapes=[FLAT, GRAM, GRAM, FLAT],
         compiler_params=pltpu.CompilerParams(vmem_limit_bytes=12 << 20),
         cost_estimate=pl.CostEstimate(flops=1 << 30, bytes_accessed=2 << 20, transcendentals=0),
@@ -171,8 +232,8 @@
     )(base, turned, following, part)
 
 
-def along_kernel(row_step, base_ref, own_ref, low_ref, same_ref, other_ref, cost_ref,
-                 pair_s, vert_s):
+def along_kernel(row_step, base_ref, own_ref, high_ref, low_ref, same_ref, other_ref,
+                 cost_ref, code_ref, all_ref, pair_s, vert_s):
     base = base_ref[0]
     half = H // 2
     size = C * T * 2 * H + H
@@ -223,20 +284,28 @@
         vert_s[level] = jnp.zeros((ROWS, W), F32)
     for level in range(HALF):
         cost_ref[level] = low_ref[level] + vert_s[base + level] * FACTOR
-
-
-def along(row_step, base, own, low, same, other):
+    planes = [cost_ref[level] for level in range(HALF)]
+    power = power_of(largest_of(planes))
+    words = packed(planes, power)
+    put(code_ref, 0, words)
+    code_ref[HALF_WORDS : HALF_WORDS + 8, :] = power
+    all_ref[0 : HALF_WORDS + 8, :] = high_ref[...]
+    put(all_ref, HALF_WORDS + 8, words)
+    all_ref[2 * HALF_WORDS + 8 :, :] = power
+
+
+def along(row_step, base, own, high, low, same, other):
     padded = pltpu.VMEM((2 * (C * T * 2 * H + H), W), F32)
     return pl.pallas_call(
         functools.partial(along_kernel, row_step),
-        out_shape=jax.ShapeDtypeStruct((HALF, ROWS, W), F32),
-        in_specs=[SMEM] + [VMEM] * 4,
-        out_specs=VMEM,
+        out_shape=(jax.ShapeDtypeStruct((HALF, ROWS, W), F32), coded(HALF), coded(NDISP, 2)),
+        in_specs=[SMEM] + [VMEM] * 5,
+        out_specs=(VMEM,) * 3,
         scratch_shapes=[padded, pltpu.VMEM((H + 4, ROWS, W), F32)],
         compiler_params=pltpu.CompilerParams(vmem_limit_bytes=12 << 20),
         cost_estimate=pl.CostEstimate(flops=2 << 30, bytes_accessed=2 << 20, transcendentals=0),
         name="along",
-    )(base, own, low, same, other)
+    )(base, own, high, low, same, other)
 
 
 def prepare_kernel(last, one_hbm, bias_hbm, two_hbm, one_ref, bias_ref, two_ref,
@@ -322,38 +391,33 @@
     return jnp.where(lane == W - 1, 0.0, pltpu.roll(x, W - 1, 1))
 
 
-def convolve(pairs, frames, one_ref, bias_ref, two_ref, scratch, write):
-    steps = HALF // LEVELS
+def convolve(pair, frames, one_ref, bias_ref, two_ref, scratch, write):
+    steps = NDISP // LEVELS
     spread, middle = scratch[:2], scratch[2:]
 
     def split(s):
         target = spread[s % 2]
         for k in range(LEVELS):
-            x = jnp.concatenate([ref[s * LEVELS + k] for ref in frames], axis=0)
+            x = jnp.concatenate([plane(s * LEVELS + k) for plane in frames], axis=0)
             for e, value in enumerate((from_left(x), x, from_right(x))):
                 for q, part in enumerate(two_parts(value)):
-                    target[e, q, 0 : len(frames) * ROWS, k * W : (k + 1) * W] = part
+                    target[e, q, :, k * W : (k + 1) * W] = part
 
     def first(s):
         source, target = spread[s % 2], middle[s % 2]
-        for place, pair in enumerate(pairs):
-            rows = slice(ROWS * place, ROWS * place + 2 * ROWS)
-            total = None
-            for e in range(3):
-                parts = [source[e, q, rows, :] for q in range(2)]
-                term = jnp.dot(one_ref[e, pair], jnp.concatenate(parts * 2, axis=0),
-                               preferred_element_type=F32)
-                total = term if total is None else total + term
-            bias = bias_ref[W * pair : W * pair + W, :]
-            hidden = jnp.maximum(total + jnp.concatenate([bias] * LEVELS, axis=1), 0.0)
-            for q, part in enumerate(two_parts(hidden)):
-                target[place, q * W : (q + 1) * W, :] = part
+        total = None
+        for e in range(3):
+            parts = [source[e, q] for q in range(2)]
+            term = jnp.dot(one_ref[e, pair], jnp.concatenate(parts * 2, axis=0),
+                           preferred_element_type=F32)
+            total = term if total is None else total + term
+        bias = bias_ref[W * pair : W * pair + W, :]
+        hidden = jnp.maximum(total + jnp.concatenate([bias] * LEVELS, axis=1), 0.0)
+        for q, part in enumerate(two_parts(hidden)):
+            target[q * W : (q + 1) * W, :] = part
 
     def second(s):
-        total = None
-        for place, pair in enumerate(pairs):
-            term = jnp.dot(two_ref[pair], middle[s % 2][place], preferred_element_type=F32)
-            total = term if total is None else total + term
+        total = jnp.dot(two_ref[pair], middle[s % 2][...], preferred_element_type=F32)
         both = total[: 3 * ROWS] + total[3 * ROWS :]
         for k in range(LEVELS):
             mine = both[:, k * W : (k + 1) * W]
@@ -370,54 +434,50 @@
             second(s - 1)
 
 
-def softened(agg_ref, lowest):
-    largest = agg_ref[0]
-    for j in range(1, HALF):
-        largest = jnp.maximum(largest, agg_ref[j])
+def early_kernel(low_code, high_code, low_ref, high_ref, one_ref, bias_ref, two_ref, agg_ref,
+                 before_s, *scratch):
+    unpack(low_code, 0, HALF_WORDS, before_s, 0, HALF)
+    unpack(high_code, 0, HALF_WORDS, before_s, HALF, HALF)
+
+    def cost(j):
+        return low_ref[j] if j < HALF else high_ref[j - HALF]
+
+    def write(j, value):
+        agg_ref[j] = cost(j) + value
+
+    convolve(0, (lambda j: before_s[j], cost), one_ref, bias_ref, two_ref, scratch, write)
+
+
+def late_kernel(base_ref, code_ref, low_ref, high_ref, early_ref, one_ref, bias_ref, two_ref,
+                out_ref, after_s, agg_s, *scratch):
+    unpack(code_ref, HALF_WORDS + 8, 2 * HALF_WORDS + 8, after_s, 0, HALF)
+    unpack(code_ref, 0, HALF_WORDS, after_s, HALF, HALF)
+
+    def write(j, value):
+        agg_s[j] = early_ref[j] + value
+
+    def cost(j):
+        return low_ref[j] if j < HALF else high_ref[j - HALF]
+
+    convolve(1, (cost, lambda j: after_s[j]), one_ref, bias_ref, two_ref, scratch, write)
+
+    base = base_ref[0].astype(F32)
+    largest = agg_s[0]
+    for j in range(1, NDISP):
+        largest = jnp.maximum(largest, agg_s[j])
     weight = jnp.zeros((ROWS, W), F32)
     moment = jnp.zeros((ROWS, W), F32)
-    for j in range(HALF):
-        e = jnp.exp(agg_ref[j] - largest)
+    for j in range(NDISP):
+        e = jnp.exp(agg_s[j] - largest)
         weight = weight + e
-        moment = moment + e * (lowest + float(j))
-    return largest, weight, moment
-
-
-def high_kernel(base_ref, before_ref, cost_ref, after_ref, one_ref, bias_ref, two_ref, out_ref,
-                agg_s, *scratch):
-    def write(j, value):
-        agg_s[j] = cost_ref[j] + value
-
-    convolve((0, 1), (before_ref, cost_ref, after_ref), one_ref, bias_ref, two_ref, scratch, write)
-    lowest = base_ref[0].astype(F32) + float(HALF)
-    for k, value in enumerate(softened(agg_s, lowest)):
-        out_ref[k] = value
-
-
-def early_kernel(before_ref, cost_ref, one_ref, bias_ref, two_ref, agg_ref, *scratch):
-    def write(j, value):
-        agg_ref[j] = cost_ref[j] + value
-
-    convolve((0,), (before_ref, cost_ref), one_ref, bias_ref, two_ref, scratch, write)
-
-
-def late_kernel(base_ref, cost_ref, after_ref, one_ref, bias_ref, two_ref, early_ref, high_ref,
-                out_ref, agg_s, *scratch):
-    def write(j, value):
-        agg_s[j] = early_ref[j] + value
-
-    convolve((1,), (cost_ref, after_ref), one_ref, bias_ref, two_ref, scratch, write)
-    largest, weight, moment = softened(agg_s, base_ref[0].astype(F32))
-    top = jnp.maximum(largest, high_ref[0])
-    low_part, high_part = jnp.exp(largest - top), jnp.exp(high_ref[0] - top)
-    weight = weight * low_part + high_ref[1] * high_part
-    out_ref[...] = (moment * low_part + high_ref[2] * high_part) / weight
-
-
-def conv_call(kernel, out_shape, in_specs, pairs, own_sums, *operands):
-    spread = pltpu.VMEM((3, 2, (pairs + 1) * ROWS, LEVELS * W), BF16)
-    middle = pltpu.VMEM((pairs, 2 * W, LEVELS * W), BF16)
-    sums = [pltpu.VMEM((HALF, ROWS, W), F32)] if own_sums else []
+        moment = moment + e * (base + float(j))
+    out_ref[...] = moment / weight
+
+
+def conv_call(kernel, out_shape, in_specs, sums, *operands):
+    sums = [pltpu.VMEM((levels, ROWS, W), F32) for levels in sums]
+    spread = pltpu.VMEM((3, 2, 2 * ROWS, LEVELS * W), BF16)
+    middle = pltpu.VMEM((2 * W, LEVELS * W), BF16)
     return pl.pallas_call(
         kernel,
         out_shape=jax.ShapeDtypeStruct(out_shape, F32),
@@ -426,7 +486,7 @@
         scratch_shapes=sums + [spread, spread, middle, middle],
         compiler_params=pltpu.CompilerParams(vmem_limit_bytes=12 << 20),
         cost_estimate=pl.CostEstimate(
-            flops=pairs << 30, bytes_accessed=1 << 20, transcendentals=0),
+            flops=1 << 30, bytes_accessed=1 << 20, transcendentals=0),
     )(*operands)
 
 
@@ -440,19 +500,19 @@
     other = swapped(same, lambda k: k ^ (2 * row_step))
     turned, part = with_near(
         disparity_base, pltpu.with_memory_space_constraint(own, pltpu.HBM), near)
-    cost_high, low = with_next(disparity_base, turned, following, part)
-    before_high = shifted_along(cost_high, "tm", 1)
-    after_high = shifted_along(cost_high, "tm", -1)
-    cost_low = along(row_step, disparity_base, own, low, same, other)
-    before_low = shifted_along(cost_low, "tm", 1)
-    after_low = shifted_along(cost_low, "tm", -1)
+    cost_high, low, code_high = with_next(disparity_base, turned, following, part)
+    before_high = shifted_along(code_high, "tm", 1)
+    cost_low, code_low, code_all = along(
+        row_step, disparity_base, own, code_high, low, same, other)
+    before_low = shifted_along(code_low, "tm", 1)
+    after = shifted_along(code_all, "tm", -1)
     matrices = prepare(lax.axis_size("tm") - 1, conv_one, conv_bias, conv_two)
-    high = conv_call(high_kernel, (3, ROWS, W), [SMEM] + [VMEM] * 6, 2, True,
-                     disparity_base, before_high, cost_high, after_high, *matrices)
-    early = conv_call(early_kernel, (HALF, ROWS, W), [VMEM] * 5, 1, False,
-                      before_low, cost_low, *matrices)
-    out = conv_call(late_kernel, (ROWS, W), [SMEM] + [VMEM] * 7, 1, True,
-                    disparity_base, cost_low, after_low, *matrices, early, high)
+    early = conv_call(early_kernel, (NDISP, ROWS, W), [VMEM] * 7, (NDISP,),
+                      before_low, before_high, cost_low, cost_high,
+                      *matrices)
+    out = conv_call(late_kernel, (ROWS, W), [SMEM] + [VMEM] * 7, (NDISP, NDISP),
+                    disparity_base, after, cost_low, cost_high, early,
+                    *matrices)
     return out.reshape(1, T, H, W)
 
 

time: 52.6 us -> 56.4 us (1.072)
  the two profiles are of different devices: /device:TPU:30 before, /device:TPU:6 now
where the time goes in v3:
time: 56.4 us; the launch traced here: 56 us
  starting transfers between devices  29.2 us (52%)
  waiting for transfers between devices  13.5 us (24%)
  Pallas kernels  12.5 us (22%)
  between operations  0.77 us (1%)
    ppermute x3, starting transfers between devices, shifted_along(): return lax.ppermute(block, axis, route)  16.1 us
    ppermute x4, starting transfers between devices, swapped(): lax.ppermute(block, 'cam', [(partner(k), k) for k in range(lax.axis_size(...  13.1 us
    ppermute x3, waiting for transfers between devices, shifted_along(): return lax.ppermute(block, axis, route)  9.89 us
    pallas_call x2, Pallas kernels, conv_call(): pl.pallas_call(kernel, out_shape=jax.ShapeDtypeStruct(out_shape, F32), in...  4.94 us
    ppermute x4, waiting for transfers between devices, swapped(): lax.ppermute(block, 'cam', [(partner(k), k) for k in range(lax.axis_size(...  3.65 us
    pallas_call x1, Pallas kernels, with_near(): pl.pallas_call(near_kernel, out_shape=(jax.ShapeDtypeStruct((ROWS * C, W)...  2.49 us
    pallas_call x1, Pallas kernels, with_next(): pl.pallas_call(next_kernel, out_shape=(half, half, coded(HALF)), in_specs...  1.79 us
    pallas_call x1, Pallas kernels, prepare(): pl.pallas_call(functools.partial(prepare_kernel, last), out_shape=(jax.Sh...  1.78 us
  transfers between devices with their start and end apart: 7, of which 4 were waited for; matrix products, arithmetic and copies ran while one was open for 0% of the time, Pallas kernels for 15%

profile of v3, /device:TPU:6, one launch (start us, length us, event | category | flops | bytes accessed | tf_op | source)
XLA Modules:
  0.0 56.0 jit_solution(3116779953116577754)
XLA Ops:
  0.0 5.1 %collective-permute-start.2 = (bf16[32,2,16,128]{3,2,1,0:T(8,128)(2,1)}, bf16[32,2,16,128]{3,2,1,0:T(8,128)(2,1)S(1)}, u32[]{:S(2)}, u32[]{:S(2)}) collective-permute-start(bf16[32,2,16,128]{3,2,1,0:T(8,128)(2,1)} %bitcast.4), channel_id=1, source_target_pairs={{4,0},{5,1},{6,2},{7,3},{0,4},{1,5},{2,6},{3,7},{12,8},{13,9},{14,... | collective-permute-start | bytes 786440 | tf_op jit(solution)/shard_map/ppermute | solution.py:34
  5.1 1.9 %collective-permute-start = (bf16[32,2,16,128]{3,2,1,0:T(8,128)(2,1)}, bf16[32,2,16,128]{3,2,1,0:T(8,128)(2,1)S(1)}, u32[]{:S(2)}, u32[]{:S(2)}) collective-permute-start(bf16[32,2,16,128]{3,2,1,0:T(8,128)(2,1)} %bitcast.5), channel_id=1, source_target_pairs={{1,0},{0,1},{3,2},{2,3},{5,4},{4,5},{7,6},{6,7},{9,8},{8,9},{11,10... | collective-permute-start | bytes 786440 | tf_op jit(solution)/shard_map/ppermute | solution.py:34
  7.0 3.3 %collective-permute-start.1 = (bf16[32,2,16,128]{3,2,1,0:T(8,128)(2,1)}, bf16[32,2,16,128]{3,2,1,0:T(8,128)(2,1)S(1)}, u32[]{:S(2)}, u32[]{:S(2)}) collective-permute-start(bf16[32,2,16,128]{3,2,1,0:T(8,128)(2,1)} %bitcast.6), channel_id=1, source_target_pairs={{15,0},{2,1},{1,2},{4,3},{3,4},{6,5},{5,6},{8,7},{7,8},{10,9},{9,1... | collective-permute-start | bytes 786440 | tf_op jit(solution)/shard_map/ppermute | solution.py:34
  10.4 1.3 %collective-permute-done.2.same_ref = bf16[32,2,16,128]{3,2,1,0:T(8,128)(2,1)S(1)} collective-permute-done((bf16[32,2,16,128]{3,2,1,0:T(8,128)(2,1)}, bf16[32,2,16,128]{3,2,1,0:T(8,128)(2,1)S(1)}, u32[]{:S(2)}, u32[]{:S(2)}) %collective-permute-start.2) | collective-permute-done | bytes 262176 | tf_op jit(solution)/shard_map/ppermute | solution.py:34
  11.6 2.7 %collective-permute-start.3 = (bf16[32,2,16,128]{3,2,1,0:T(8,128)(2,1)S(1)}, bf16[32,2,16,128]{3,2,1,0:T(8,128)(2,1)S(1)}, u32[]{:S(2)}, u32[]{:S(2)}) collective-permute-start(bf16[32,2,16,128]{3,2,1,0:T(8,128)(2,1)S(1)} %collective-permute-done.2.same_ref), channel_id=1, source_target_pairs={{8,0},{9,1},{10,2},{11,3},{12,4},{13,5},{14,6},{15,7},{0,8},{1,9},... | collective-permute-start | bytes 786440 | tf_op jit(solution)/shard_map/ppermute | solution.py:34
  15.0 0.0 collective-permute-done.near_ref
  15.0 2.5 %with_near.1 = (bf16[1024,128]{1,0:T(8,128)(2,1)S(1)}, f32[32,32,128]{2,1,0:T(8,128)S(1)}) custom-call(s32[1]{0:T(128)S(6)} %copy.6.base_ref, bf16[32,2,16,128]{3,2,1,0:T(8,128)(2,1)} %bitcast.7, bf16[32,2,16,128]{3,2,1,0:T(8,128)(2,1)S(1)} %collective-permute-done.near_ref), custom_call_target="tpu_custom_call" | custom-call | flops 1073741824 | bytes 2097152 | tf_op jit(solution)/shard_map/with_near/pallas_call | solution.py:207
  17.5 0.0 collective-permute-done.1.next_ref
  17.5 0.0 copy-start
  17.6 1.8 %with_next.1 = (f32[16,32,128]{2,1,0:T(8,128)S(1)}, f32[16,32,128]{2,1,0:T(8,128)S(1)}, s32[392,128]{1,0:T(8,128)S(1)}) custom-call(s32[1]{0:T(128)S(6)} %copy.6.base_ref, bf16[1024,128]{1,0:T(8,128)(2,1)S(1)} %get-tuple-element.16.turned_ref, bf16[32,2,16,128]{3,2,1,0:T(8,128)(2,1)S(1)} %collective-permute-done.1.next_ref, ...), custom_call_target="tpu_custom_call" | custom-call | flops 1073741824 | bytes 2097152 | tf_op jit(solution)/shard_map/with_next/pallas_call | solution.py:223
  19.3 2.4 %collective-permute-done.3.other_ref = bf16[32,2,16,128]{3,2,1,0:T(8,128)(2,1)S(1)} collective-permute-done((bf16[32,2,16,128]{3,2,1,0:T(8,128)(2,1)S(1)}, bf16[32,2,16,128]{3,2,1,0:T(8,128)(2,1)S(1)}, u32[]{:S(2)}, u32[]{:S(2)}) %collective-permute-start.3) | collective-permute-done | bytes 262176 | tf_op jit(solution)/shard_map/ppermute | solution.py:34
  21.7 0.0 copy-done
  21.7 1.5 %along.1 = (f32[16,32,128]{2,1,0:T(8,128)S(1)}, s32[392,128]{1,0:T(8,128)S(1)}, s32[784,128]{1,0:T(8,128)S(1)}) custom-call(s32[1]{0:T(128)S(6)} %copy.6.base_ref, bf16[32,2,16,128]{3,2,1,0:T(8,128)(2,1)S(1)} %bitcast.8, s32[392,128]{1,0:T(8,128)S(1)} %get-tuple-element.18.high_ref, f32[16,32,128]{2,1,0:T(8,128)S(1)} %get-tuple-element.19.low_ref, ...), custom_call_target="tpu_custom_call" | custom-call | flops 2147483648 | bytes 2097152 | tf_op jit(solution)/shard_map/along/pallas_call | solution.py:299
  23.2 12.2 %collective-permute-start.4 = (s32[784,128]{1,0:T(8,128)S(1)}, s32[784,128]{1,0:T(8,128)S(1)}, u32[]{:S(2)}, u32[]{:S(2)}) collective-permute-start(s32[784,128]{1,0:T(8,128)S(1)} %get-tuple-element.20), channel_id=1, source_target_pairs={{16,0},{32,16},{48,32},{64,48},{80,64},{96,80},{112,96},{128,112},... | collective-permute-start | bytes 1204232 | tf_op jit(solution)/shard_map/ppermute | solution.py:40
  35.5 1.9 %collective-permute-start.6 = (s32[392,128]{1,0:T(8,128)S(1)}, s32[392,128]{1,0:T(8,128)S(1)}, u32[]{:S(2)}, u32[]{:S(2)}) collective-permute-start(s32[392,128]{1,0:T(8,128)S(1)} %get-tuple-element.18.high_ref), channel_id=1, source_target_pairs={{0,16},{16,32},{32,48},{48,64},{64,80},{80,96},{96,112},{112,128},... | collective-permute-start | bytes 602120 | tf_op jit(solution)/shard_map/ppermute | solution.py:40
  37.4 1.9 %collective-permute-start.5 = (s32[392,128]{1,0:T(8,128)S(1)}, s32[392,128]{1,0:T(8,128)S(1)}, u32[]{:S(2)}, u32[]{:S(2)}) collective-permute-start(s32[392,128]{1,0:T(8,128)S(1)} %get-tuple-element.23), channel_id=1, source_target_pairs={{0,16},{16,32},{32,48},{48,64},{64,80},{80,96},{96,112},{112,128},... | collective-permute-start | bytes 602120 | tf_op jit(solution)/shard_map/ppermute | solution.py:40
  39.3 1.8 %prepare.1 = (bf16[3,2,128,256]{3,2,1,0:T(8,128)(2,1)S(1)}, f32[256,128]{1,0:T(8,128)S(1)}, bf16[2,192,256]{2,1,0:T(8,128)(2,1)S(1)}) custom-call(f32[3,3,4,3]{3,2,1,0:T(4,128)} %bitcast.9, f32[4]{0:T(128)} %bias_hbm.1, f32[3,3,4,3]{3,2,1,0:T(4,128)} %bitcast.10), custom_call_target="tpu_custom_call" | custom-call | flops 1048576 | bytes 524288 | tf_op jit(solution)/shard_map/prepare/pallas_call | solution.py:366
  41.1 7.7 %collective-permute-done.6.high_code = s32[392,128]{1,0:T(8,128)S(1)} collective-permute-done((s32[392,128]{1,0:T(8,128)S(1)}, s32[392,128]{1,0:T(8,128)S(1)}, u32[]{:S(2)}, u32[]{:S(2)}) %collective-permute-start.6) | collective-permute-done | bytes 200736 | tf_op jit(solution)/shard_map/ppermute | solution.py:40
  48.8 2.2 %collective-permute-done.5.low_code = s32[392,128]{1,0:T(8,128)S(1)} collective-permute-done((s32[392,128]{1,0:T(8,128)S(1)}, s32[392,128]{1,0:T(8,128)S(1)}, u32[]{:S(2)}, u32[]{:S(2)}) %collective-permute-start.5) | collective-permute-done | bytes 200736 | tf_op jit(solution)/shard_map/ppermute | solution.py:40
  51.0 2.1 %shard_map.55.early_ref = f32[32,32,128]{2,1,0:T(8,128)S(1)} custom-call(s32[392,128]{1,0:T(8,128)S(1)} %collective-permute-done.5.low_code, s32[392,128]{1,0:T(8,128)S(1)} %collective-permute-done.6.high_code, f32[16,32,128]{2,1,0:T(8,128)S(1)} %get-tuple-element.21.low_ref, f32[16,32,128]{2,1,0:T(8,128)S(1)} %get-tuple-element.22.high_ref, ...), custom_call_target="tpu_custom_call" | custom-call | flops 1073741824 | bytes 1048576 | tf_op jit(solution)/shard_map/pallas_call | solution.py:481
  53.1 0.0 collective-permute-done.4.code_ref
  53.1 2.8 %shard_map.56 = f32[32,128]{1,0:T(8,128)} custom-call(s32[1]{0:T(128)S(6)} %copy.6.base_ref, s32[784,128]{1,0:T(8,128)S(1)} %collective-permute-done.4.code_ref, f32[16,32,128]{2,1,0:T(8,128)S(1)} %get-tuple-element.21.low_ref, f32[16,32,128]{2,1,0:T(8,128)S(1)} %get-tuple-element.22.high_ref, f32[32,32,128]{2,1,0:T(8,128)S(1)} %shard_map.55.early_ref, ...), custom_call_target="tpu_custom_call" | custom-call | flops 1073741824 | bytes 1048576 | tf_op jit(solution)/shard_map/pallas_call | solution.py:481
Async XLA Ops:
  0.0 11.6 %collective-permute-start.2 = (bf16[32,2,16,128]{3,2,1,0:T(8,128)(2,1)}, bf16[32,2,16,128]{3,2,1,0:T(8,128)(2,1)S(1)}, u32[]{:S(2)}, u32[]{:S(2)}) collective-permute-start(bf16[32,2,16,128]{3,2,1,0:T(8,128)(2,1)} %bitcast.4), channel_id=1, source_target_pairs={{4,0},{5,1},{6,2},{7,3},{0,4},{1,5},{2,6},{3,7},{12,8},{13,9},{14,... | collective-permute-start | bytes 786440 | tf_op jit(solution)/shard_map/ppermute | solution.py:34
  5.1 9.9 %collective-permute-start = (bf16[32,2,16,128]{3,2,1,0:T(8,128)(2,1)}, bf16[32,2,16,128]{3,2,1,0:T(8,128)(2,1)S(1)}, u32[]{:S(2)}, u32[]{:S(2)}) collective-permute-start(bf16[32,2,16,128]{3,2,1,0:T(8,128)(2,1)} %bitcast.5), channel_id=1, source_target_pairs={{1,0},{0,1},{3,2},{2,3},{5,4},{4,5},{7,6},{6,7},{9,8},{8,9},{11,10... | collective-permute-start | bytes 786440 | tf_op jit(solution)/shard_map/ppermute | solution.py:34
  7.0 10.5 %collective-permute-start.1 = (bf16[32,2,16,128]{3,2,1,0:T(8,128)(2,1)}, bf16[32,2,16,128]{3,2,1,0:T(8,128)(2,1)S(1)}, u32[]{:S(2)}, u32[]{:S(2)}) collective-permute-start(bf16[32,2,16,128]{3,2,1,0:T(8,128)(2,1)} %bitcast.6), channel_id=1, source_target_pairs={{15,0},{2,1},{1,2},{4,3},{3,4},{6,5},{5,6},{8,7},{7,8},{10,9},{9,1... | collective-permute-start | bytes 786440 | tf_op jit(solution)/shard_map/ppermute | solution.py:34
  11.6 10.1 %collective-permute-start.3 = (bf16[32,2,16,128]{3,2,1,0:T(8,128)(2,1)S(1)}, bf16[32,2,16,128]{3,2,1,0:T(8,128)(2,1)S(1)}, u32[]{:S(2)}, u32[]{:S(2)}) collective-permute-start(bf16[32,2,16,128]{3,2,1,0:T(8,128)(2,1)S(1)} %collective-permute-done.2.same_ref), channel_id=1, source_target_pairs={{8,0},{9,1},{10,2},{11,3},{12,4},{13,5},{14,6},{15,7},{0,8},{1,9},... | collective-permute-start | bytes 786440 | tf_op jit(solution)/shard_map/ppermute | solution.py:34
  17.5 4.2 %copy-start = (bf16[1,32,2,16,128]{4,3,2,1,0:T(8,128)(2,1)S(1)}, bf16[1,32,2,16,128]{4,3,2,1,0:T(8,128)(2,1)}, u32[]{:S(2)}) copy-start(bf16[1,32,2,16,128]{4,3,2,1,0:T(8,128)(2,1)} %param.5) | copy-start | bytes 786436
  23.2 29.9 %collective-permute-start.4 = (s32[784,128]{1,0:T(8,128)S(1)}, s32[784,128]{1,0:T(8,128)S(1)}, u32[]{:S(2)}, u32[]{:S(2)}) collective-permute-start(s32[784,128]{1,0:T(8,128)S(1)} %get-tuple-element.20), channel_id=1, source_target_pairs={{16,0},{32,16},{48,32},{64,48},{80,64},{96,80},{112,96},{128,112},... | collective-permute-start | bytes 1204232 | tf_op jit(solution)/shard_map/ppermute | solution.py:40
  35.5 13.4 %collective-permute-start.6 = (s32[392,128]{1,0:T(8,128)S(1)}, s32[392,128]{1,0:T(8,128)S(1)}, u32[]{:S(2)}, u32[]{:S(2)}) collective-permute-start(s32[392,128]{1,0:T(8,128)S(1)} %get-tuple-element.18.high_ref), channel_id=1, source_target_pairs={{0,16},{16,32},{32,48},{48,64},{64,80},{80,96},{96,112},{112,128},... | collective-permute-start | bytes 602120 | tf_op jit(solution)/shard_map/ppermute | solution.py:40
  37.4 13.6 %collective-permute-start.5 = (s32[392,128]{1,0:T(8,128)S(1)}, s32[392,128]{1,0:T(8,128)S(1)}, u32[]{:S(2)}, u32[]{:S(2)}) collective-permute-start(s32[392,128]{1,0:T(8,128)S(1)} %get-tuple-element.23), channel_id=1, source_target_pairs={{0,16},{16,32},{32,48},{48,64},{64,80},{80,96},{96,112},{112,128},... | collective-permute-start | bytes 602120 | tf_op jit(solution)/shard_map/ppermute | solution.py:40

commit v4 on v3

--- a/solution.py
+++ b/solution.py
@@ -56,16 +56,19 @@
 
 
 def power_of(top):
-    power = jnp.full((8, W), LOWEST_POWER - 1, jnp.int32)
-    for k in range(LOWEST_POWER, HIGHEST_POWER + 1):
-        power = jnp.where(top >= 2.0**k, k, power)
-    return power
+    counts = [
+        (top >= 2.0**k).astype(jnp.int32) for k in range(LOWEST_POWER, HIGHEST_POWER + 1)
+    ]
+    while len(counts) > 1:
+        counts = [sum(counts[i : i + 2]) for i in range(0, len(counts), 2)]
+    return counts[0] + (LOWEST_POWER - 1)
 
 
 def by_power(power, sign, bits):
+    steps = power - (LOWEST_POWER - 1)
     factor = jnp.full((8, W), 2.0 ** (sign * (bits - LOWEST_POWER + 1)), F32)
-    for k in range(LOWEST_POWER, HIGHEST_POWER + 1):
-        factor = jnp.where(power >= k, 2.0 ** (sign * (bits - k)), factor)
+    for bit in range(6):
+        factor = factor * jnp.where((steps & (1 << bit)) != 0, 2.0 ** (-sign * (1 << bit)), 1.0)
     return jnp.concatenate([factor] * (ROWS // 8), axis=0)
 
 
@@ -82,14 +85,23 @@
     return words
 
 
-def unpack(source, start, power_at, target, place, levels):
-    factor = by_power(source[power_at : power_at + 8, :], -1, 22)
-    for i in range(0, levels, 4):
-        at = start + i // 4 * 3 * ROWS
-        words = [source[at + k * ROWS : at + (k + 1) * ROWS, :] for k in range(3)]
-        last = ((words[2] & 255) << 24) | ((words[1] & 255) << 16) | ((words[0] & 255) << 8)
-        for k, q in enumerate([word >> 8 for word in words] + [last >> 8]):
-            target[place + i + k] = q.astype(F32) * factor
+def unpacked(places):
+    factors = [by_power(ref[at : at + 8, :], -1, 22) for ref, _, at in places]
+    held = {}
+
+    def plane(j):
+        group = j // 4
+        if group not in held:
+            ref, start, _ = places[j // HALF]
+            at = start + (group - j // HALF * (HALF // 4)) * 3 * ROWS
+            words = [ref[at + k * ROWS : at + (k + 1) * ROWS, :] for k in range(3)]
+            last = ((words[2] & 255) << 24) | ((words[1] & 255) << 16) | ((words[0] & 255) << 8)
+            held[group] = [
+                (q >> 8).astype(F32) * factors[j // HALF] for q in (*words, last)
+            ]
+        return held[group][j % 4]
+
+    return plane
 
 
 def put(target, start, words):
@@ -435,9 +447,8 @@
 
 
 def early_kernel(low_code, high_code, low_ref, high_ref, one_ref, bias_ref, two_ref, agg_ref,
-                 before_s, *scratch):
-    unpack(low_code, 0, HALF_WORDS, before_s, 0, HALF)
-    unpack(high_code, 0, HALF_WORDS, before_s, HALF, HALF)
+                 *scratch):
+    before = unpacked(((low_code, 0, HALF_WORDS), (high_code, 0, HALF_WORDS)))
 
     def cost(j):
         return low_ref[j] if j < HALF else high_ref[j - HALF]
@@ -445,13 +456,13 @@
     def write(j, value):
         agg_ref[j] = cost(j) + value
 
-    convolve(0, (lambda j: before_s[j], cost), one_ref, bias_ref, two_ref, scratch, write)
+    convolve(0, (before, cost), one_ref, bias_ref, two_ref, scratch, write)
 
 
 def late_kernel(base_ref, code_ref, low_ref, high_ref, early_ref, one_ref, bias_ref, two_ref,
-                out_ref, after_s, agg_s, *scratch):
-    unpack(code_ref, HALF_WORDS + 8, 2 * HALF_WORDS + 8, after_s, 0, HALF)
-    unpack(code_ref, 0, HALF_WORDS, after_s, HALF, HALF)
+                out_ref, agg_s, *scratch):
+    after = unpacked(
+        ((code_ref, HALF_WORDS + 8, 2 * HALF_WORDS + 8), (code_ref, 0, HALF_WORDS)))
 
     def write(j, value):
         agg_s[j] = early_ref[j] + value
@@ -459,7 +470,7 @@
     def cost(j):
         return low_ref[j] if j < HALF else high_ref[j - HALF]
 
-    convolve(1, (cost, lambda j: after_s[j]), one_ref, bias_ref, two_ref, scratch, write)
+    convolve(1, (cost, after), one_ref, bias_ref, two_ref, scratch, write)
 
     base = base_ref[0].astype(F32)
     largest = agg_s[0]
@@ -507,10 +518,10 @@
     before_low = shifted_along(code_low, "tm", 1)
     after = shifted_along(code_all, "tm", -1)
     matrices = prepare(lax.axis_size("tm") - 1, conv_one, conv_bias, conv_two)
-    early = conv_call(early_kernel, (NDISP, ROWS, W), [VMEM] * 7, (NDISP,),
+    early = conv_call(early_kernel, (NDISP, ROWS, W), [VMEM] * 7, (),
                       before_low, before_high, cost_low, cost_high,
                       *matrices)
-    out = conv_call(late_kernel, (ROWS, W), [SMEM] + [VMEM] * 7, (NDISP, NDISP),
+    out = conv_call(late_kernel, (ROWS, W), [SMEM] + [VMEM] * 7, (NDISP,),
                     disparity_base, after, cost_low, cost_high, early,
                     *matrices)
     return out.reshape(1, T, H, W)

time: 56.4 us -> 56.3 us (level)
  no operation moved by 1% of the time
where the time goes in v4:
time: 56.3 us; the launch traced here: 55.9 us
  starting transfers between devices  29.2 us (52%)
  waiting for transfers between devices  13.6 us (24%)
  Pallas kernels  12.4 us (22%)
  between operations  0.77 us (1%)
    ppermute x3, starting transfers between devices, shifted_along(): return lax.ppermute(block, axis, route)  16.1 us
    ppermute x4, starting transfers between devices, swapped(): lax.ppermute(block, 'cam', [(partner(k), k) for k in range(lax.axis_size(...  13.1 us
    ppermute x3, waiting for transfers between devices, shifted_along(): return lax.ppermute(block, axis, route)  9.89 us
    pallas_call x2, Pallas kernels, conv_call(): pl.pallas_call(kernel, out_shape=jax.ShapeDtypeStruct(out_shape, F32), in...  4.88 us
    ppermute x4, waiting for transfers between devices, swapped(): lax.ppermute(block, 'cam', [(partner(k), k) for k in range(lax.axis_size(...  3.67 us
    pallas_call x1, Pallas kernels, with_near(): pl.pallas_call(near_kernel, out_shape=(jax.ShapeDtypeStruct((ROWS * C, W)...  2.49 us
    pallas_call x1, Pallas kernels, prepare(): pl.pallas_call(functools.partial(prepare_kernel, last), out_shape=(jax.Sh...  1.78 us
    pallas_call x1, Pallas kernels, with_next(): pl.pallas_call(next_kernel, out_shape=(half, half, coded(HALF)), in_specs...  1.77 us
  transfers between devices with their start and end apart: 7, of which 4 were waited for; matrix products, arithmetic and copies ran while one was open for 0% of the time, Pallas kernels for 15%

profile of v4, /device:TPU:6, one launch (start us, length us, event | category | flops | bytes accessed | tf_op | source)
XLA Modules:
  0.0 55.9 jit_solution(13682297381839702057)
XLA Ops:
  0.0 5.1 %collective-permute-start.2 = (bf16[32,2,16,128]{3,2,1,0:T(8,128)(2,1)}, bf16[32,2,16,128]{3,2,1,0:T(8,128)(2,1)S(1)}, u32[]{:S(2)}, u32[]{:S(2)}) collective-permute-start(bf16[32,2,16,128]{3,2,1,0:T(8,128)(2,1)} %bitcast.4), channel_id=1, source_target_pairs={{4,0},{5,1},{6,2},{7,3},{0,4},{1,5},{2,6},{3,7},{12,8},{13,9},{14,... | collective-permute-start | bytes 786440 | tf_op jit(solution)/shard_map/ppermute | solution.py:34
  5.1 1.9 %collective-permute-start = (bf16[32,2,16,128]{3,2,1,0:T(8,128)(2,1)}, bf16[32,2,16,128]{3,2,1,0:T(8,128)(2,1)S(1)}, u32[]{:S(2)}, u32[]{:S(2)}) collective-permute-start(bf16[32,2,16,128]{3,2,1,0:T(8,128)(2,1)} %bitcast.5), channel_id=1, source_target_pairs={{1,0},{0,1},{3,2},{2,3},{5,4},{4,5},{7,6},{6,7},{9,8},{8,9},{11,10... | collective-permute-start | bytes 786440 | tf_op jit(solution)/shard_map/ppermute | solution.py:34
  7.0 3.3 %collective-permute-start.1 = (bf16[32,2,16,128]{3,2,1,0:T(8,128)(2,1)}, bf16[32,2,16,128]{3,2,1,0:T(8,128)(2,1)S(1)}, u32[]{:S(2)}, u32[]{:S(2)}) collective-permute-start(bf16[32,2,16,128]{3,2,1,0:T(8,128)(2,1)} %bitcast.6), channel_id=1, source_target_pairs={{15,0},{2,1},{1,2},{4,3},{3,4},{6,5},{5,6},{8,7},{7,8},{10,9},{9,1... | collective-permute-start | bytes 786440 | tf_op jit(solution)/shard_map/ppermute | solution.py:34
  10.4 1.3 %collective-permute-done.2.same_ref = bf16[32,2,16,128]{3,2,1,0:T(8,128)(2,1)S(1)} collective-permute-done((bf16[32,2,16,128]{3,2,1,0:T(8,128)(2,1)}, bf16[32,2,16,128]{3,2,1,0:T(8,128)(2,1)S(1)}, u32[]{:S(2)}, u32[]{:S(2)}) %collective-permute-start.2) | collective-permute-done | bytes 262176 | tf_op jit(solution)/shard_map/ppermute | solution.py:34
  11.6 2.7 %collective-permute-start.3 = (bf16[32,2,16,128]{3,2,1,0:T(8,128)(2,1)S(1)}, bf16[32,2,16,128]{3,2,1,0:T(8,128)(2,1)S(1)}, u32[]{:S(2)}, u32[]{:S(2)}) collective-permute-start(bf16[32,2,16,128]{3,2,1,0:T(8,128)(2,1)S(1)} %collective-permute-done.2.same_ref), channel_id=1, source_target_pairs={{8,0},{9,1},{10,2},{11,3},{12,4},{13,5},{14,6},{15,7},{0,8},{1,9},... | collective-permute-start | bytes 786440 | tf_op jit(solution)/shard_map/ppermute | solution.py:34
  15.0 0.0 collective-permute-done.near_ref
  15.0 2.5 %with_near.1 = (bf16[1024,128]{1,0:T(8,128)(2,1)S(1)}, f32[32,32,128]{2,1,0:T(8,128)S(1)}) custom-call(s32[1]{0:T(128)S(6)} %copy.6.base_ref, bf16[32,2,16,128]{3,2,1,0:T(8,128)(2,1)} %bitcast.7, bf16[32,2,16,128]{3,2,1,0:T(8,128)(2,1)S(1)} %collective-permute-done.near_ref), custom_call_target="tpu_custom_call" | custom-call | flops 1073741824 | bytes 2097152 | tf_op jit(solution)/shard_map/with_near/pallas_call | solution.py:219
  17.5 0.0 collective-permute-done.1.next_ref
  17.5 0.0 copy-start
  17.6 1.8 %with_next.1 = (f32[16,32,128]{2,1,0:T(8,128)S(1)}, f32[16,32,128]{2,1,0:T(8,128)S(1)}, s32[392,128]{1,0:T(8,128)S(1)}) custom-call(s32[1]{0:T(128)S(6)} %copy.6.base_ref, bf16[1024,128]{1,0:T(8,128)(2,1)S(1)} %get-tuple-element.16.turned_ref, bf16[32,2,16,128]{3,2,1,0:T(8,128)(2,1)S(1)} %collective-permute-done.1.next_ref, ...), custom_call_target="tpu_custom_call" | custom-call | flops 1073741824 | bytes 2097152 | tf_op jit(solution)/shard_map/with_next/pallas_call | solution.py:235
  19.3 2.4 %collective-permute-done.3.other_ref = bf16[32,2,16,128]{3,2,1,0:T(8,128)(2,1)S(1)} collective-permute-done((bf16[32,2,16,128]{3,2,1,0:T(8,128)(2,1)S(1)}, bf16[32,2,16,128]{3,2,1,0:T(8,128)(2,1)S(1)}, u32[]{:S(2)}, u32[]{:S(2)}) %collective-permute-start.3) | collective-permute-done | bytes 262176 | tf_op jit(solution)/shard_map/ppermute | solution.py:34
  21.7 0.0 copy-done
  21.7 1.5 %along.1 = (f32[16,32,128]{2,1,0:T(8,128)S(1)}, s32[392,128]{1,0:T(8,128)S(1)}, s32[784,128]{1,0:T(8,128)S(1)}) custom-call(s32[1]{0:T(128)S(6)} %copy.6.base_ref, bf16[32,2,16,128]{3,2,1,0:T(8,128)(2,1)S(1)} %bitcast.8, s32[392,128]{1,0:T(8,128)S(1)} %get-tuple-element.18.high_ref, f32[16,32,128]{2,1,0:T(8,128)S(1)} %get-tuple-element.19.low_ref, ...), custom_call_target="tpu_custom_call" | custom-call | flops 2147483648 | bytes 2097152 | tf_op jit(solution)/shard_map/along/pallas_call | solution.py:311
  23.2 12.2 %collective-permute-start.4 = (s32[784,128]{1,0:T(8,128)S(1)}, s32[784,128]{1,0:T(8,128)S(1)}, u32[]{:S(2)}, u32[]{:S(2)}) collective-permute-start(s32[784,128]{1,0:T(8,128)S(1)} %get-tuple-element.20), channel_id=1, source_target_pairs={{16,0},{32,16},{48,32},{64,48},{80,64},{96,80},{112,96},{128,112},... | collective-permute-start | bytes 1204232 | tf_op jit(solution)/shard_map/ppermute | solution.py:40
  35.5 1.9 %collective-permute-start.6 = (s32[392,128]{1,0:T(8,128)S(1)}, s32[392,128]{1,0:T(8,128)S(1)}, u32[]{:S(2)}, u32[]{:S(2)}) collective-permute-start(s32[392,128]{1,0:T(8,128)S(1)} %get-tuple-element.18.high_ref), channel_id=1, source_target_pairs={{0,16},{16,32},{32,48},{48,64},{64,80},{80,96},{96,112},{112,128},... | collective-permute-start | bytes 602120 | tf_op jit(solution)/shard_map/ppermute | solution.py:40
  37.4 1.9 %collective-permute-start.5 = (s32[392,128]{1,0:T(8,128)S(1)}, s32[392,128]{1,0:T(8,128)S(1)}, u32[]{:S(2)}, u32[]{:S(2)}) collective-permute-start(s32[392,128]{1,0:T(8,128)S(1)} %get-tuple-element.23), channel_id=1, source_target_pairs={{0,16},{16,32},{32,48},{48,64},{64,80},{80,96},{96,112},{112,128},... | collective-permute-start | bytes 602120 | tf_op jit(solution)/shard_map/ppermute | solution.py:40
  39.3 1.8 %prepare.1 = (bf16[3,2,128,256]{3,2,1,0:T(8,128)(2,1)S(1)}, f32[256,128]{1,0:T(8,128)S(1)}, bf16[2,192,256]{2,1,0:T(8,128)(2,1)S(1)}) custom-call(f32[3,3,4,3]{3,2,1,0:T(4,128)} %bitcast.9, f32[4]{0:T(128)} %bias_hbm.1, f32[3,3,4,3]{3,2,1,0:T(4,128)} %bitcast.10), custom_call_target="tpu_custom_call" | custom-call | flops 1048576 | bytes 524288 | tf_op jit(solution)/shard_map/prepare/pallas_call | solution.py:378
  41.1 7.7 %collective-permute-done.6.high_code = s32[392,128]{1,0:T(8,128)S(1)} collective-permute-done((s32[392,128]{1,0:T(8,128)S(1)}, s32[392,128]{1,0:T(8,128)S(1)}, u32[]{:S(2)}, u32[]{:S(2)}) %collective-permute-start.6) | collective-permute-done | bytes 200736 | tf_op jit(solution)/shard_map/ppermute | solution.py:40
  48.8 2.2 %collective-permute-done.5.low_code = s32[392,128]{1,0:T(8,128)S(1)} collective-permute-done((s32[392,128]{1,0:T(8,128)S(1)}, s32[392,128]{1,0:T(8,128)S(1)}, u32[]{:S(2)}, u32[]{:S(2)}) %collective-permute-start.5) | collective-permute-done | bytes 200736 | tf_op jit(solution)/shard_map/ppermute | solution.py:40
  51.0 2.1 %shard_map.55.early_ref = f32[32,32,128]{2,1,0:T(8,128)S(1)} custom-call(s32[392,128]{1,0:T(8,128)S(1)} %collective-permute-done.5.low_code, s32[392,128]{1,0:T(8,128)S(1)} %collective-permute-done.6.high_code, f32[16,32,128]{2,1,0:T(8,128)S(1)} %get-tuple-element.21.low_ref, f32[16,32,128]{2,1,0:T(8,128)S(1)} %get-tuple-element.22.high_ref, ...), custom_call_target="tpu_custom_call" | custom-call | flops 1073741824 | bytes 1048576 | tf_op jit(solution)/shard_map/pallas_call | solution.py:492
  53.1 0.0 collective-permute-done.4.code_ref
  53.1 2.8 %shard_map.56 = f32[32,128]{1,0:T(8,128)} custom-call(s32[1]{0:T(128)S(6)} %copy.6.base_ref, s32[784,128]{1,0:T(8,128)S(1)} %collective-permute-done.4.code_ref, f32[16,32,128]{2,1,0:T(8,128)S(1)} %get-tuple-element.21.low_ref, f32[16,32,128]{2,1,0:T(8,128)S(1)} %get-tuple-element.22.high_ref, f32[32,32,128]{2,1,0:T(8,128)S(1)} %shard_map.55.early_ref, ...), custom_call_target="tpu_custom_call" | custom-call | flops 1073741824 | bytes 1048576 | tf_op jit(solution)/shard_map/pallas_call | solution.py:492
Async XLA Ops:
  0.0 11.6 %collective-permute-start.2 = (bf16[32,2,16,128]{3,2,1,0:T(8,128)(2,1)}, bf16[32,2,16,128]{3,2,1,0:T(8,128)(2,1)S(1)}, u32[]{:S(2)}, u32[]{:S(2)}) collective-permute-start(bf16[32,2,16,128]{3,2,1,0:T(8,128)(2,1)} %bitcast.4), channel_id=1, source_target_pairs={{4,0},{5,1},{6,2},{7,3},{0,4},{1,5},{2,6},{3,7},{12,8},{13,9},{14,... | collective-permute-start | bytes 786440 | tf_op jit(solution)/shard_map/ppermute | solution.py:34
  5.1 9.9 %collective-permute-start = (bf16[32,2,16,128]{3,2,1,0:T(8,128)(2,1)}, bf16[32,2,16,128]{3,2,1,0:T(8,128)(2,1)S(1)}, u32[]{:S(2)}, u32[]{:S(2)}) collective-permute-start(bf16[32,2,16,128]{3,2,1,0:T(8,128)(2,1)} %bitcast.5), channel_id=1, source_target_pairs={{1,0},{0,1},{3,2},{2,3},{5,4},{4,5},{7,6},{6,7},{9,8},{8,9},{11,10... | collective-permute-start | bytes 786440 | tf_op jit(solution)/shard_map/ppermute | solution.py:34
  7.0 10.5 %collective-permute-start.1 = (bf16[32,2,16,128]{3,2,1,0:T(8,128)(2,1)}, bf16[32,2,16,128]{3,2,1,0:T(8,128)(2,1)S(1)}, u32[]{:S(2)}, u32[]{:S(2)}) collective-permute-start(bf16[32,2,16,128]{3,2,1,0:T(8,128)(2,1)} %bitcast.6), channel_id=1, source_target_pairs={{15,0},{2,1},{1,2},{4,3},{3,4},{6,5},{5,6},{8,7},{7,8},{10,9},{9,1... | collective-permute-start | bytes 786440 | tf_op jit(solution)/shard_map/ppermute | solution.py:34
  11.6 10.1 %collective-permute-start.3 = (bf16[32,2,16,128]{3,2,1,0:T(8,128)(2,1)S(1)}, bf16[32,2,16,128]{3,2,1,0:T(8,128)(2,1)S(1)}, u32[]{:S(2)}, u32[]{:S(2)}) collective-permute-start(bf16[32,2,16,128]{3,2,1,0:T(8,128)(2,1)S(1)} %collective-permute-done.2.same_ref), channel_id=1, source_target_pairs={{8,0},{9,1},{10,2},{11,3},{12,4},{13,5},{14,6},{15,7},{0,8},{1,9},... | collective-permute-start | bytes 786440 | tf_op jit(solution)/shard_map/ppermute | solution.py:34
  17.5 4.2 %copy-start = (bf16[1,32,2,16,128]{4,3,2,1,0:T(8,128)(2,1)S(1)}, bf16[1,32,2,16,128]{4,3,2,1,0:T(8,128)(2,1)}, u32[]{:S(2)}) copy-start(bf16[1,32,2,16,128]{4,3,2,1,0:T(8,128)(2,1)} %param.5) | copy-start | bytes 786436
  23.2 29.9 %collective-permute-start.4 = (s32[784,128]{1,0:T(8,128)S(1)}, s32[784,128]{1,0:T(8,128)S(1)}, u32[]{:S(2)}, u32[]{:S(2)}) collective-permute-start(s32[784,128]{1,0:T(8,128)S(1)} %get-tuple-element.20), channel_id=1, source_target_pairs={{16,0},{32,16},{48,32},{64,48},{80,64},{96,80},{112,96},{128,112},... | collective-permute-start | bytes 1204232 | tf_op jit(solution)/shard_map/ppermute | solution.py:40
  35.5 13.4 %collective-permute-start.6 = (s32[392,128]{1,0:T(8,128)S(1)}, s32[392,128]{1,0:T(8,128)S(1)}, u32[]{:S(2)}, u32[]{:S(2)}) collective-permute-start(s32[392,128]{1,0:T(8,128)S(1)} %get-tuple-element.18.high_ref), channel_id=1, source_target_pairs={{0,16},{16,32},{32,48},{48,64},{64,80},{80,96},{96,112},{112,128},... | collective-permute-start | bytes 602120 | tf_op jit(solution)/shard_map/ppermute | solution.py:40
  37.4 13.6 %collective-permute-start.5 = (s32[392,128]{1,0:T(8,128)S(1)}, s32[392,128]{1,0:T(8,128)S(1)}, u32[]{:S(2)}, u32[]{:S(2)}) collective-permute-start(s32[392,128]{1,0:T(8,128)S(1)} %get-tuple-element.23), channel_id=1, source_target_pairs={{0,16},{16,32},{32,48},{48,64},{64,80},{80,96},{96,112},{112,128},... | collective-permute-start | bytes 602120 | tf_op jit(solution)/shard_map/ppermute | solution.py:40
